TPU v7x, 128 devices: a whole 4x4x4 slice. The times are simulated.
128 devices in a mesh: query: 4 (over x_hi, core), corpus: 32 (over y, x_lo, z).
Axes of the slice: x: 4 (x_hi: 2, x_lo: 2; x = x_hi * 2 + x_lo), y: 4, z: 4, core: 2. Of those that a mesh axis runs over, the one named last changes fastest.
Arguments:
- passages: bfloat16 [4096, 768], P('corpus'), may hold values from -64 to 64
- queries: bfloat16 [8192, 768], P(('query', 'corpus')), may hold values from -64 to 64
- codebook: float32 [96, 8, 256], replicated, may hold values from -6 to 6
Outputs:
- divergence: float32 [8192], P('query')
- codebook_grad: float32 [96, 8, 256], replicated
All inputs are finite; a program needn't handle non-finite values.
Results may differ from a plain program's by a relative error of at most 0.0053.
Values may be sent and summed in bfloat16 or wider, within the bound.
A program may use at most 64 MiB of HBM per device.

v0:
```python
import math

import jax
import jax.numpy as jnp
from jax import lax
from jax.sharding import PartitionSpec as P

ASSIGN_TEMP = 2.0
HIGHEST = lax.Precision.HIGHEST


def soft_assign(row_block, codebook):
    row_count = row_block.shape[0]
    subspaces, sub_width, codewords = codebook.shape
    pieces = row_block.astype(jnp.float32).reshape(row_count, subspaces, sub_width)
    cross_term = jnp.einsum("rms,msk->rmk", pieces, codebook, precision=HIGHEST)
    distance = (
        jnp.sum(pieces * pieces, axis=-1)[:, :, None]
        - 2.0 * cross_term
        + jnp.sum(codebook * codebook, axis=1)[None]
    )
    weights = jax.nn.softmax(-distance / ASSIGN_TEMP, axis=-1)
    rebuilt = jnp.einsum("rmk,msk->rms", weights, codebook, precision=HIGHEST)
    return rebuilt.reshape(row_count, subspaces * sub_width)


def assign_grad(row_block, codebook, cotangent):
    _, pullback = jax.vjp(lambda book_value: soft_assign(row_block, book_value), codebook)
    return pullback(cotangent)[0]


def rebuild_set(row_set, codebook):
    row_total = row_set.shape[0]
    feature_width = row_set.shape[1]
    block_rows = math.gcd(row_total, 64)
    blocked = row_set.reshape(row_total // block_rows, block_rows, feature_width)
    rebuilt = lax.map(lambda row_block: soft_assign(row_block, codebook), blocked)
    return rebuilt.reshape(row_total, feature_width).astype(jnp.bfloat16)


def codebook_terms(row_set, codebook, cotangent):
    row_total = row_set.shape[0]
    feature_width = row_set.shape[1]
    block_rows = math.gcd(row_total, 64)
    blocked = row_set.reshape(row_total // block_rows, block_rows, feature_width)
    grad_blocks = cotangent.reshape(row_total // block_rows, block_rows, feature_width)

    def add_block(running, block_pair):
        return (running + assign_grad(block_pair[0], codebook, block_pair[1]), None)

    summed, _ = lax.scan(add_block, jnp.zeros_like(codebook), (blocked, grad_blocks))
    return summed


def local(passages, queries, codebook):
    row_total = passages.shape[0]
    feature_width = passages.shape[1]
    score_scale = float(feature_width) ** (-0.5)
    kl_weight = row_total * lax.axis_size("corpus") / 64.0
    rebuilt = rebuild_set(passages, codebook)
    gathered = lax.all_gather(queries, "corpus", axis=0, tiled=True)
    dims_rows = (((1,), (1,)), ((), ()))
    teacher = (
        lax.dot_general(gathered, passages, dims_rows, preferred_element_type=jnp.float32)
        * score_scale
    )
    student = (
        lax.dot_general(gathered, rebuilt, dims_rows, preferred_element_type=jnp.float32)
        * score_scale
    )
    top_teacher, top_student = lax.pmax(
        (jnp.max(teacher, axis=1), jnp.max(student, axis=1)), "corpus"
    )
    exp_teacher = jnp.exp(teacher - top_teacher[:, None])
    exp_student = jnp.exp(student - top_student[:, None])
    total_teacher, total_student, cross_total = lax.psum(
        (
            jnp.sum(exp_teacher, axis=1),
            jnp.sum(exp_student, axis=1),
            jnp.sum(exp_teacher * (teacher - student), axis=1),
        ),
        "corpus",
    )
    divergence = (
        cross_total / total_teacher
        - top_teacher
        - jnp.log(total_teacher)
        + top_student
        + jnp.log(total_student)
    )
    prob_teacher = exp_teacher / total_teacher[:, None]
    prob_student = exp_student / total_student[:, None]
    grad_scores = ((prob_student - prob_teacher) * (kl_weight * score_scale)).astype(jnp.bfloat16)
    grad_rebuilt = lax.dot_general(
        grad_scores, gathered, (((0,), (0,)), ((), ())), preferred_element_type=jnp.float32
    )
    partial_grad = codebook_terms(passages, codebook, grad_rebuilt)
    codebook_grad = lax.psum(partial_grad, ("query", "corpus"))
    return (divergence, codebook_grad)


def solution(mesh):
    placed = (P("corpus", None), P(("query", "corpus"), None), P())
    return jax.shard_map(
        local, mesh=mesh, in_specs=placed, out_specs=(P("query"), P()), check_vma=False
    )
```

profile of v0, /device:TPU:1, one launch (start us, length us, event | category | flops | bytes accessed | tf_op | source)
XLA Modules:
  0.0 733.8 jit_solution(74351580033379264)
XLA Ops:
  11.1 29.9 %while.25 = (s32[]{:T(128)}, bf16[2,64,768]{2,1,0:T(8,128)(2,1)S(1)}, bf16[2,64,768]{1,2,0:T(8,128)(2,1)S(1)}, f32[96,8,256]{2,1,0:T(8,128)}, f32[96,256]{1,0:T(8,128)}, /*index=5*/s32[]{:T(128)}) while((s32[]{:T(128)}, bf16[2,64,768]{2,1,0:T(8,128)(2,1)S(1)}, bf16[2,64,768]{1,2,0:T(8,128)(2,1)S(1)}, f32[96,8,256]{2,1,0:T(8,128)}, ...), condition=%wide.region_7.8_spmd, body=%wide.region_3.7_spmd.sunk | while | flops 317847552 | bytes 24674420 | solution.py:37
  11.3 5.8 fusion.112
  19.0 6.9 fusion.114
  26.2 5.8 fusion.112
  33.9 6.9 fusion.114
  41.7 104.6 %all-gather.2.cloned.1.call-done = bf16[2048,768]{1,0:T(8,128)(2,1)} async-done(((bf16[64,768]{1,0:T(8,128)(2,1)}), bf16[2048,768]{1,0:T(8,128)(2,1)}) %all-gather.2.cloned.1.call-update) | async-done | bytes 3145744 | tf_op jit(solution)/shard_map/all_gather | solution.py:61
  146.3 4.2 fusion.79
  152.6 129.5 %all-reduce.1 = (f32[2048]{0:T(1024)}, f32[2048]{0:T(1024)}) all-reduce(f32[2048]{0:T(1024)S(1)} %get-tuple-element.207, f32[2048]{0:T(1024)S(1)} %get-tuple-element.209), channel_id=1, replica_groups=mesh['query'=4,'corpus'=32] {'corpus'}, use_global_device_ids=true, to_apply=%region_1.0 | all-reduce | flops 4096 | bytes 32768 | tf_op jit(solution)/shard_map/pmax | solution.py:71
  284.6 125.0 %all-reduce = (f32[2048]{0:T(1024)}, f32[2048]{0:T(1024)}, f32[2048]{0:T(1024)}) all-reduce(f32[2048]{0:T(1024)} %get-tuple-element.171, f32[2048]{0:T(1024)S(1)} %get-tuple-element.170, f32[2048]{0:T(1024)S(1)} %get-tuple-element.169), channel_id=1, replica_groups=mesh['query'=4,'corpus'=32] {'corpus'}, use_global_device_ids=true, to_apply=%region_15.16 | all-reduce | flops 6144 | bytes 49152 | tf_op jit(solution)/shard_map/psum | solution.py:76
  409.7 3.1 fusion.75
  412.8 92.1 %while.26 = (s32[]{:T(128)}, f32[96,8,256]{2,1,0:T(8,128)}, f32[2,64,768]{2,1,0:T(8,128)}, bf16[2,64,768]{1,2,0:T(8,128)(2,1)S(1)}, f32[96,8,256]{2,1,0:T(8,128)}, /*index=5*/f32[96,256]{1,0:T(8,128)}, s32[]{:T(128)}, s32[]{:T(128)}) while((s32[]{:T(128)}, f32[96,8,256]{2,1,0:T(8,128)}, f32[2,64,768]{2,1,0:T(8,128)}, ...), condition=%wide.region_22.23_spmd.clone, body=%wide.region_16.22_spmd.clone.sunk | while | flops 682371072 | bytes 111157472 | solution.py:51
  413.0 5.6 fusion.121
  421.2 3.7 fusion.122
  425.2 10.8 %fusion.123 = (f32[64,96]{0,1:T(8,128)S(1)}, f32[96,64,256]{2,1,0:T(8,128)S(1)}) fusion(f32[64,96]{0,1:T(8,128)S(1)} %multiply_divide_fusion.2, f32[64,96]{0,1:T(8,128)S(1)} %get-tuple-element.289, f32[96,256]{1,0:T(8,128)} %get-tuple-element.334, f32[96,64,256]{2,1,0:T(8,128)} %copy-done, f32[64,96]{0,1:T(8,128)S(1)} %multiply_reduce_fusion.6, ...), kind=kOutput, calls=%fused_computation.22.clone.1 | convolution fusion | flops 165144576 | bytes 13762560 | tf_op jit(solution)/shard_map/while/body/eval_jaxpr/transpose(jvp(rmk,msk->rms))/dot_general | solution.py:23
  436.1 8.9 %fusion.125 = f32[96,8,256]{2,1,0:T(8,128)} fusion(f32[96,64,256]{2,1,0:T(8,128)S(1)} %get-tuple-element.291, f32[96,64,256]{2,1,0:T(8,128)S(1)} %bitcast.147, f32[96,64]{1,0:T(8,128)S(1)} %bitcast.150, f32[96,256]{1,0:T(8,128)} %get-tuple-element.334, f32[96,64]{1,0:T(8,128)S(1)} %bitcast.149, f32[96,64]{1,0:T(8,128)S(1)} %get-tuple-element.293, ...), kind=kOutput, calls=%fused_computation.27.clone.1 | convolution fusion | flops 165150720 | bytes 13860868 | tf_op jit(solution)/shard_map/while/body/eval_jaxpr/transpose(jvp(rms,msk->rmk))/dot_general | solution.py:16
  445.0 5.8 fusion.126
  450.8 8.1 %fusion.127 = f32[96,8,256]{2,1,0:T(8,128)} fusion(f32[96,8,256]{2,1,0:T(8,128)} %fusion.125, f32[64,96]{0,1:T(8,128)S(1)} %fusion.122, f32[96,8,256]{2,1,0:T(8,128)} %get-tuple-element.322, f32[96,8,256]{2,1,0:T(8,128)} %get-tuple-element.333, f32[1,64,768]{1,2,0:T(8,128)S(1)} %copy.20, f32[96,256]{1,0:T(8,128)S(1)} %neg.84, pred[]{:T(512)S(6)} %compare.3, ...), kind=kOutput, calls=%fused_computation.54.clone.1 | convolution fusion | flops 163184640 | bytes 9904129 | tf_op jit(solution)/shard_map/while/body/eval_jaxpr/transpose(jvp(rmk,msk->rms))/dot_general | solution.py:23
  459.0 5.6 fusion.121
  467.2 3.7 fusion.122
  471.2 10.8 %fusion.123 = (f32[64,96]{0,1:T(8,128)S(1)}, f32[96,64,256]{2,1,0:T(8,128)S(1)}) fusion(f32[64,96]{0,1:T(8,128)S(1)} %multiply_divide_fusion.2, f32[64,96]{0,1:T(8,128)S(1)} %get-tuple-element.289, f32[96,256]{1,0:T(8,128)} %get-tuple-element.334, f32[96,64,256]{2,1,0:T(8,128)} %copy-done, f32[64,96]{0,1:T(8,128)S(1)} %multiply_reduce_fusion.6, ...), kind=kOutput, calls=%fused_computation.22.clone.1 | convolution fusion | flops 165144576 | bytes 13762560 | tf_op jit(solution)/shard_map/while/body/eval_jaxpr/transpose(jvp(rmk,msk->rms))/dot_general | solution.py:23
  482.0 8.9 %fusion.125 = f32[96,8,256]{2,1,0:T(8,128)} fusion(f32[96,64,256]{2,1,0:T(8,128)S(1)} %get-tuple-element.291, f32[96,64,256]{2,1,0:T(8,128)S(1)} %bitcast.147, f32[96,64]{1,0:T(8,128)S(1)} %bitcast.150, f32[96,256]{1,0:T(8,128)} %get-tuple-element.334, f32[96,64]{1,0:T(8,128)S(1)} %bitcast.149, f32[96,64]{1,0:T(8,128)S(1)} %get-tuple-element.293, ...), kind=kOutput, calls=%fused_computation.27.clone.1 | convolution fusion | flops 165150720 | bytes 13860868 | tf_op jit(solution)/shard_map/while/body/eval_jaxpr/transpose(jvp(rms,msk->rmk))/dot_general | solution.py:16
  491.0 5.8 fusion.126
  496.7 8.2 %fusion.127 = f32[96,8,256]{2,1,0:T(8,128)} fusion(f32[96,8,256]{2,1,0:T(8,128)} %fusion.125, f32[64,96]{0,1:T(8,128)S(1)} %fusion.122, f32[96,8,256]{2,1,0:T(8,128)} %get-tuple-element.322, f32[96,8,256]{2,1,0:T(8,128)} %get-tuple-element.333, f32[1,64,768]{1,2,0:T(8,128)S(1)} %copy.20, f32[96,256]{1,0:T(8,128)S(1)} %neg.84, pred[]{:T(512)S(6)} %compare.3, ...), kind=kOutput, calls=%fused_computation.54.clone.1 | convolution fusion | flops 163184640 | bytes 9904129 | tf_op jit(solution)/shard_map/while/body/eval_jaxpr/transpose(jvp(rmk,msk->rms))/dot_general | solution.py:23
  505.6 219.3 %all-reduce.4.cloned.1.call-done = f32[96,8,256]{2,1,0:T(8,128)} async-done(((f32[96,8,256]{2,1,0:T(8,128)}), f32[96,8,256]{2,1,0:T(8,128)}) %all-reduce.4.cloned.1.call-update) | async-done | bytes 786448 | tf_op jit(solution)/shard_map/psum | solution.py:98
  (70 shorter events, 22.3 us)
Async XLA Ops:
  7.2 139.1 %all-gather.2.cloned.1.call-start = ((), (), s32[]{:S(2)}) async-start(), calls=%async_computation | async-start | bytes 3244032 | tf_op jit(solution)/shard_map/all_gather | solution.py:61
  7.9 717.0 %all-reduce.4.cloned.1.call-start = ((), (), s32[]{:S(2)}) async-start(), calls=%async_computation.1 | async-start | bytes 1572864 | tf_op jit(solution)/shard_map/psum | solution.py:98
  11.3 7.7 %copy-start.3 = (f32[96,8,256]{2,1,0:T(8,128)S(1)}, f32[96,8,256]{2,1,0:T(8,128)}, u32[]{:S(2)}) copy-start(f32[96,8,256]{2,1,0:T(8,128)} %get-tuple-element.310) | copy-start | bytes 2359300 | tf_op jit(solution)/shard_map/while
  26.2 7.7 %copy-start.3 = (f32[96,8,256]{2,1,0:T(8,128)S(1)}, f32[96,8,256]{2,1,0:T(8,128)}, u32[]{:S(2)}) copy-start(f32[96,8,256]{2,1,0:T(8,128)} %get-tuple-element.310) | copy-start | bytes 2359300 | tf_op jit(solution)/shard_map/while
  41.0 0.7 copy-start.4
  146.2 4.2 copy-start.1
  146.3 4.2 copy-start.5
  412.8 92.2 %copy-start.6 = (f32[2048]{0:T(1024)S(1)}, f32[2048]{0:T(1024)}, u32[]{:S(2)}) copy-start(f32[2048]{0:T(1024)} %get-tuple-element.197) | copy-start | bytes 24580
  412.8 92.2 %copy-start.7 = (f32[2048]{0:T(1024)S(1)}, f32[2048]{0:T(1024)}, u32[]{:S(2)}) copy-start(f32[2048]{0:T(1024)} %get-tuple-element.198) | copy-start | bytes 24580
  412.8 92.2 %copy-start.8 = (f32[2048]{0:T(1024)S(1)}, f32[2048]{0:T(1024)}, u32[]{:S(2)}) copy-start(f32[2048]{0:T(1024)} %get-tuple-element.194) | copy-start | bytes 24580
  412.8 92.2 %copy-start.9 = (f32[2048]{0:T(1024)S(1)}, f32[2048]{0:T(1024)}, u32[]{:S(2)}) copy-start(f32[2048]{0:T(1024)} %get-tuple-element.195) | copy-start | bytes 24580
  412.8 92.2 %copy-start.10 = (f32[2048]{0:T(1024)S(1)}, f32[2048]{0:T(1024)}, u32[]{:S(2)}) copy-start(f32[2048]{0:T(1024)} %get-tuple-element.196) | copy-start | bytes 24580
  413.0 12.0 %copy-start.2 = (f32[2,64,768]{2,1,0:T(8,128)S(1)}, f32[2,64,768]{2,1,0:T(8,128)}, u32[]{:S(2)}) copy-start(f32[2,64,768]{2,1,0:T(8,128)} %get-tuple-element.331) | copy-start | bytes 1179652 | tf_op jit(solution)/shard_map/while
  418.5 2.7 copy-start
  425.0 11.0 %slice-start = ((s8[6291456]{0:T(1024)(128)(4,1)}), s8[2097152]{0:T(1024)(128)(4,1)S(1)}, s32[]{:S(2)}) async-start(s8[6291456]{0:T(1024)(128)(4,1)} %bitcast.146), calls=%async_computation.2 | async-start | bytes 4194304 | tf_op jit(solution)/shard_map/while
  425.2 10.9 %slice-start.1 = ((s8[6291456]{0:T(1024)(128)(4,1)}), s8[4194304]{0:T(1024)(128)(4,1)S(1)}, s32[]{:S(2)}) async-start(s8[6291456]{0:T(1024)(128)(4,1)} %bitcast.146), calls=%async_computation.3 | async-start | bytes 8388608 | tf_op jit(solution)/shard_map/while
  459.0 12.0 %copy-start.2 = (f32[2,64,768]{2,1,0:T(8,128)S(1)}, f32[2,64,768]{2,1,0:T(8,128)}, u32[]{:S(2)}) copy-start(f32[2,64,768]{2,1,0:T(8,128)} %get-tuple-element.331) | copy-start | bytes 1179652 | tf_op jit(solution)/shard_map/while
  464.5 2.7 copy-start
  471.0 11.0 %slice-start = ((s8[6291456]{0:T(1024)(128)(4,1)}), s8[2097152]{0:T(1024)(128)(4,1)S(1)}, s32[]{:S(2)}) async-start(s8[6291456]{0:T(1024)(128)(4,1)} %bitcast.146), calls=%async_computation.2 | async-start | bytes 4194304 | tf_op jit(solution)/shard_map/while
  471.2 10.9 %slice-start.1 = ((s8[6291456]{0:T(1024)(128)(4,1)}), s8[4194304]{0:T(1024)(128)(4,1)S(1)}, s32[]{:S(2)}) async-start(s8[6291456]{0:T(1024)(128)(4,1)} %bitcast.146), calls=%async_computation.3 | async-start | bytes 8388608 | tf_op jit(solution)/shard_map/while
Sparse Core Ops, SparseCore 0:
  9.6 136.5 all-gather.1
  505.1 219.7 all-reduce.3
where the time goes:
time: 736 us; the launch traced here: 734 us
  waiting for transfers between devices  325 us (44%)
  blocking collectives  255 us (35%)
  matrix products  102 us (14%)
  other arithmetic  28.5 us (4%)
  between operations  14.1 us (2%)
  local copies, waits for them, and re-layouts  9.92 us (1%)
    psum x1, waiting for transfers between devices, local(): codebook_grad = lax.psum(partial_grad, ('query', 'corpus'))  219 us
    pmax x1, blocking collectives, local(): lax.pmax((jnp.max(teacher, axis=1), jnp.max(student, axis=1)), 'corpus')  130 us
    psum x1, blocking collectives, local(): lax.psum((jnp.sum(exp_teacher, axis=1), jnp.sum(exp_student, axis=1), jnp...  125 us
    all_gather x1, waiting for transfers between devices, local(): gathered = lax.all_gather(queries, 'corpus', axis=0, tiled=True)  105 us
    dot_general x6, matrix products, soft_assign(): rebuilt = jnp.einsum('rmk,msk->rms', weights, codebook, precision=HIGHEST)  51.7 us
    dot_general x6, matrix products, soft_assign(): cross_term = jnp.einsum('rms,msk->rmk', pieces, codebook, precision=HIGHEST)  40.6 us
  transfers between devices with their start and end apart: 2, of which 2 were waited for; matrix products, arithmetic and copies ran while one was open for 5% of the time, Pallas kernels for 0%

commit v1 on v0

v1 whole, which is shorter than its diff:
```python
import functools

import jax
import jax.numpy as jnp
from jax import lax
from jax.experimental import pallas as pl
from jax.experimental.pallas import tpu as pltpu
from jax.sharding import PartitionSpec as P

MESH = pl.DeviceIdType.MESH
F32 = jnp.float32
BF16 = jnp.bfloat16
NT = (((1,), (1,)), ((), ()))
NN = (((1,), (0,)), ((), ()))

D = 768
SUB = 8
CODES = 256
QB = 64
PB = 128
PLANE = 16
TILE = 128
GROUPS = 16
ROWS = 256
QN = 1024
N_SEM = 136


def split3(value):
    high = value.astype(BF16)
    rest = value - high.astype(F32)
    mid = rest.astype(BF16)
    low = (rest - mid.astype(F32)).astype(BF16)
    return high, mid, low


def split2(value):
    high = value.astype(BF16)
    low = (value - high.astype(F32)).astype(BF16)
    return high, low


def dot(a, b, dims):
    return lax.dot_general(a, b, dims, preferred_element_type=F32)


def kernel(
    p_ref, q_ref, cb_ref,
    out_ref, div_ref,
    qbuf, pbuf, rbuf,
    lhs_f, lhs_b, cp3, ct, rt, a1b, a2b,
    tbuf, ebt, ebs, mloc, stat,
    gown, gsib, gsrc, rs1, rs1s, rs2, rs2s,
    acc, dcs, dcr, piece, dbuf, divb,
    send_sem, recv_sem,
):
    qi = lax.axis_index("query")
    ci = lax.axis_index("corpus")
    xh, core = qi // 2, qi % 2
    y, xl, z = ci // 8, (ci // 4) % 2, ci % 4
    x = xh * 2 + xl
    u = (x + 4 - 2 * core) % 4

    def dev(x_, y_, z_, core_):
        return ((x_ // 2) * 2 + core_, y_ * 8 + (x_ % 2) * 4 + z_)

    def dev_x(step, core_=None):
        return dev((x + step) % 4, y, z, core if core_ is None else core_)

    def dev_yz(dy, dz):
        return dev(x, (y + dy) % 4, (z + dz) % 4, core)

    sibling = dev(x, y, z, 1 - core)
    left, right = dev_x(3), dev_x(1)

    sends = []
    count = [0]

    def push(src, dst, index, device):
        copy = pltpu.make_async_remote_copy(
            src_ref=src, dst_ref=dst, send_sem=send_sem.at[len(sends)],
            recv_sem=recv_sem.at[index], device_id=device, device_id_type=MESH,
        )
        copy.start()
        sends.append(copy)

    def arrive(dst, index):
        pltpu.make_async_remote_copy(
            src_ref=dst, dst_ref=dst, send_sem=send_sem.at[0],
            recv_sem=recv_sem.at[index], device_id=sibling, device_id_type=MESH,
        ).wait_recv()

    def block(n):
        first = count[0]
        count[0] += n
        return first

    barrier = pltpu.get_barrier_semaphore()
    peers = [dev_x(s, c) for s in range(4) for c in (core, 1 - core)][1:]
    peers += [dev_yz(a, b) for a in range(4) for b in range(4)][1:]
    for peer in peers:
        pl.semaphore_signal(barrier, inc=1, device_id=peer, device_id_type=MESH)

    me = y * 4 + z
    qbuf[me] = q_ref[...]
    pbuf[xl] = p_ref[...]

    pl.semaphore_wait(barrier, len(peers))

    def gather_plane(own, piece_of, base):
        def rel(h, a, b):
            return (a, b) if h == 0 else (b, a)

        def slot(dy, dz):
            return ((y + dy) % 4) * 4 + (z + dz) % 4

        def sem(dy, dz, h, part):
            return base + (((dy % 4) * 4 + dz % 4) * 2 + h) * 2 + (part or 0)

        def send(h, a, b, part, first_axis, step):
            dy, dz = rel(h, a, b)
            sy, sz = rel(h, step, 0) if first_axis else rel(h, 0, step)
            dst = piece_of(slot(dy, dz), h, part)
            src = own(h) if (a, b) == (0, 0) else dst
            push(src, dst, sem(dy - sy, dz - sz, h, part), dev_yz(sy % 4, sz % 4))

        def wait(h, a, b, part):
            dy, dz = rel(h, a, b)
            arrive(piece_of(slot(dy, dz), h, part), sem(dy, dz, h, part))

        def wave0():
            for first in (True, False):
                for h in range(2):
                    for step in (1, 3):
                        send(h, 0, 0, None, first, step)

        def wave1():
            for h in range(2):
                for a, part, step in ((3, 0, 1), (1, 1, 3)):
                    wait(h, a, 0, None)
                    send(h, a, 0, part, True, step)
                    send(h, a, 0, None, False, 1)
                    send(h, a, 0, None, False, 3)
            for h in range(2):
                for b, part, step in ((3, 0, 1), (1, 1, 3)):
                    wait(h, 0, b, None)
                    send(h, 0, b, part, False, step)

        def wave2():
            for h in range(2):
                wait(h, 2, 0, 0)
                wait(h, 2, 0, 1)
                send(h, 2, 0, None, False, 1)
                send(h, 2, 0, None, False, 3)
            for h in range(2):
                for a in (3, 1):
                    for b, part, step in ((3, 0, 1), (1, 1, 3)):
                        wait(h, a, b, None)
                        send(h, a, b, part, False, step)

        def wave3():
            for h in range(2):
                for b, part, step in ((3, 0, 1), (1, 1, 3)):
                    wait(h, 2, b, None)
                    send(h, 2, b, part, False, step)

        def wave4():
            for h in range(2):
                for a in (0, 1, 3, 2):
                    wait(h, a, 2, 0)
                    wait(h, a, 2, 1)

        return wave0, wave1, wave2, wave3, wave4

    def q_piece(s, h, part):
        if part is None:
            return qbuf.at[s, pl.ds(32 * h, 32), :]
        return qbuf.at[s, pl.ds(32 * h + 16 * part, 16), :]

    qw = gather_plane(lambda h: q_ref.at[pl.ds(32 * h, 32), :], q_piece, block(64))
    s_p = block(1)
    x_to = (x + 3 + 2 * core) % 4
    push(p_ref, pbuf.at[xl], s_p, dev(x_to, y, z, core))
    qw[0]()

    tile = 3 * core + jnp.minimum(u, 2)
    col = pl.multiple_of(tile * TILE, TILE)
    cb = cb_ref[pl.ds(col, TILE), :]
    grouped = cb.reshape(GROUPS, SUB, CODES)
    bias = -0.5 * jnp.sum(grouped * grouped, axis=1)
    c_parts = split3(cb)
    c32 = [c.astype(F32).reshape(GROUPS, SUB, CODES) for c in c_parts]
    cp3[...] = jnp.concatenate(c32 + [jnp.zeros((GROUPS, SUB, CODES), F32)], axis=1).astype(BF16)
    cbt = cb.T
    ct[...] = cbt
    t1, t2, t3 = split3(cbt)

    def stack_rows(parts, width):
        rows = [p.astype(F32) for p in parts]
        rows.append(jnp.zeros((TILE - len(parts) * GROUPS, width), F32))
        return jnp.concatenate(rows, axis=0).T.astype(BF16)

    lane = lax.broadcasted_iota(jnp.int32, (1, 4 * TILE), 1)
    in_tile = lane % TILE
    group_id = jnp.where(
        lane < 3 * TILE, in_tile // SUB, jnp.where(in_tile < 3 * GROUPS, in_tile % GROUPS, -1)
    )
    ones48 = jnp.where(
        lax.broadcasted_iota(jnp.int32, (CODES, TILE), 1) < 3 * GROUPS, 1.0, 0.0
    ).astype(BF16)
    lhs_f[...] = jnp.concatenate([t1, t2, t3, stack_rows(split3(bias), CODES)], axis=1)
    lhs_b[...] = jnp.concatenate([t1, t1, t2, ones48], axis=1)

    qw[1]()
    arrive(pbuf.at[1 - xl], s_p)

    xt = jnp.concatenate([pbuf[0, :, pl.ds(col, TILE)], pbuf[1, :, pl.ds(col, TILE)]], axis=0)
    rhs_f = jnp.concatenate([xt, xt, xt, ones48], axis=1)

    def group_mask(i):
        return jnp.where(group_id == i, 1.0, 0.0).astype(BF16)

    def assign_step(i, carry):
        logits = dot(lhs_f[...] * group_mask(i), rhs_f, NT)
        top = jnp.max(logits, axis=0, keepdims=True)
        e = jnp.exp(logits - top)
        w = e * (1.0 / jnp.sum(e, axis=0, keepdims=True))
        w1, w2 = split2(w)
        a1b[i] = w1
        a2b[i] = w2
        got = dot(cp3[i], w1, NN) + dot(cp3[i], w2, NN)
        rt[i] = got[0:8] + got[8:16] + got[16:24]
        return carry

    lax.fori_loop(0, 8, assign_step, 0)
    qw[2]()
    lax.fori_loop(8, 16, assign_step, 0)

    mine = core * 4 + u
    rbuf[mine] = rt[...].reshape(TILE, ROWS).T.astype(BF16)

    def r_slot(step):
        return core * 4 + (u + step) % 4

    def r_sib(step):
        return (1 - core) * 4 + (u + 2 + step) % 4

    def r_half(s, part):
        return rbuf.at[s, pl.ds(128 * part, 128), :]

    s_r = block(4)
    s_rs = block(5)
    push(rbuf.at[mine], rbuf.at[mine], s_r + 0, right)
    push(rbuf.at[mine], rbuf.at[mine], s_r + 1, left)
    push(rbuf.at[mine], rbuf.at[mine], s_rs + 0, sibling)
    qw[3]()
    for step, sem_i, part, far in ((3, 0, 0, right), (1, 1, 1, left)):
        s = r_slot(step)
        arrive(rbuf.at[s], s_r + sem_i)
        push(r_half(s, part), r_half(s, part), s_r + 2 + part, far)
        push(rbuf.at[s], rbuf.at[s], s_rs + 1 + sem_i, sibling)
    qw[4]()

    p_all = pbuf[...].reshape(ROWS, D)
    scale = float(D) ** (-0.5)
    for n in range(4):
        qc = qbuf[4 * n:4 * n + 4].reshape(256, D)
        t = dot(p_all, qc, NT) * scale
        m_t = jnp.max(t, axis=0, keepdims=True)
        tbuf[n] = t
        e_t = jnp.exp(t - m_t)
        ebt[n] = e_t
        lt = m_t + jnp.log(jnp.sum(e_t, axis=0, keepdims=True))
        for k in range(2):
            mloc[2 * n + k:2 * n + k + 1, :] = m_t[:, 128 * k:128 * k + 128]
            stat[me, 2 * n + k:2 * n + k + 1, :] = lt[:, 128 * k:128 * k + 128]
        if n == 0:
            far_slot = r_slot(2)
            for part in range(2):
                arrive(r_half(far_slot, part), s_r + 2 + part)
                push(r_half(far_slot, part), r_half(far_slot, part), s_rs + 3 + part, sibling)

    arrive(rbuf.at[r_sib(0)], s_rs + 0)
    arrive(rbuf.at[r_sib(3)], s_rs + 1)
    arrive(rbuf.at[r_sib(1)], s_rs + 2)
    for part in range(2):
        arrive(r_half(r_sib(2), part), s_rs + 3 + part)

    r_all = jnp.concatenate([rbuf[k] for k in (0, 1, 2, 4, 5, 6)], axis=1)
    for n in range(4):
        qc = qbuf[4 * n:4 * n + 4].reshape(256, D)
        s = dot(r_all, qc, NT) * scale
        m_s = jnp.max(s, axis=0, keepdims=True)
        e_s = jnp.exp(s - m_s)
        ebs[n] = e_s
        ls = m_s + jnp.log(jnp.sum(e_s, axis=0, keepdims=True))
        e_t = ebt[n]
        cross = jnp.sum(e_t * (tbuf[n] - s), axis=0, keepdims=True)
        cross = cross / jnp.sum(e_t, axis=0, keepdims=True)
        for k in range(2):
            r = 2 * n + k
            mloc[8 + r:9 + r, :] = m_s[:, 128 * k:128 * k + 128]
            stat[me, 8 + r:9 + r, :] = ls[:, 128 * k:128 * k + 128]
            stat[me, 16 + r:17 + r, :] = cross[:, 128 * k:128 * k + 128]

    s_st = block(16)
    for a in range(4):
        for b in range(4):
            if (a, b) != (0, 0):
                push(stat.at[me], stat.at[me], s_st + ((4 - a) % 4) * 4 + (4 - b) % 4, dev_yz(a, b))
    for a in range(4):
        for b in range(4):
            if (a, b) != (0, 0):
                arrive(stat.at[((y + a) % 4) * 4 + (z + b) % 4], s_st + a * 4 + b)

    st = stat[...]
    lt, ls, cx = st[:, 0:8], st[:, 8:16], st[:, 16:24]
    top_t = jnp.max(lt, axis=0)
    top_s = jnp.max(ls, axis=0)
    big_t = top_t + jnp.log(jnp.sum(jnp.exp(lt - top_t[None]), axis=0))
    big_s = top_s + jnp.log(jnp.sum(jnp.exp(ls - top_s[None]), axis=0))
    cross = jnp.sum(jnp.exp(lt - big_t[None]) * cx, axis=0)
    divb[xl] = cross - big_t + big_s
    s_d = block(1)
    push(divb.at[xl], divb.at[xl], s_d, dev(x + 1 - 2 * xl, y, z, core))
    f_t = jnp.exp(mloc[0:8, :] - big_t)
    f_s = jnp.exp(mloc[8:16, :] - big_s)
    weight = (PB * 32 / 64.0) * scale

    grads = []
    for n in range(4):
        for k in range(2):
            r = 2 * n + k
            cols = slice(128 * k, 128 * k + 128)
            diff = ebs[n, :, cols] * f_s[r:r + 1] - ebt[n, :, cols] * f_t[r:r + 1]
            grads.append((diff * weight).astype(BF16))
    grad_scores = jnp.concatenate(grads, axis=1)

    def partial(group, dest):
        for k in range(3):
            at = pl.multiple_of(group * 384 + 128 * k, 128)
            qcol = qbuf[:, :, pl.ds(at, 128)].reshape(QN, 128)
            dest[k] = dot(grad_scores, qcol, NN)

    partial(1 - core, gsrc)
    s_g = block(1)
    push(gsrc, gsib, s_g, sibling)
    partial(core, gown)
    gown[3] = jnp.zeros((ROWS, TILE), F32)
    arrive(gsib, s_g)
    gown[0:3] = gown[0:3] + gsib[...]

    s_1 = block(2)
    s_2 = block(2)
    far = (u + 2) % 4
    for part, to in ((0, right), (1, left)):
        push(gown.at[far, pl.ds(128 * part, 128), :], rs1.at[part], s_1 + part, to)
    for part, to, step in ((0, right, 1), (1, left, 3)):
        d = (u + step) % 4
        arrive(rs1.at[part], s_1 + part)
        keep, add = (128, 0) if part == 0 else (0, 128)
        rs2s[part, pl.ds(keep, 128), :] = gown[d, pl.ds(keep, 128), :]
        rs2s[part, pl.ds(add, 128), :] = gown[d, pl.ds(add, 128), :] + rs1[part]
        push(rs2s.at[part], rs2.at[part], s_2 + part, to)
    arrive(rs2.at[0], s_2)
    arrive(rs2.at[1], s_2 + 1)
    g = gown[u] + rs2[0] + rs2[1]

    g1, g2 = split2(g)
    gt = g.T
    inner = jnp.sum((gt * rt[...].reshape(TILE, ROWS)).reshape(GROUPS, SUB, ROWS), axis=1)
    rhs_b = jnp.concatenate([g1, g2, g1, stack_rows(split3(-inner), ROWS)], axis=1)
    g12 = jnp.concatenate([g1, g2], axis=1)
    xo = jnp.concatenate([xt, jnp.full((ROWS, TILE), 1.0, BF16)], axis=1)
    lane_group = lax.broadcasted_iota(jnp.int32, (1, TILE), 1) // SUB

    def grad_step(i, carry):
        diff = dot(lhs_b[...] * group_mask(i), rhs_b, NT)
        w1 = a1b[i]
        w2 = a2b[i]
        d1, d2 = split2((w1.astype(F32) + w2.astype(F32)) * diff)
        o1 = dot(w1, g12, NN)
        o2 = dot(w2, g1, NN)
        o3 = dot(d1, xo, NN) + dot(d2, xo, NN)
        val = o1[:, :TILE] + o1[:, TILE:] + o2 + o3[:, :TILE] - ct[...] * o3[:, TILE:]
        acc[...] = jnp.where(lane_group == i, val, acc[...])
        return carry

    acc[...] = jnp.zeros_like(acc)
    lax.fori_loop(0, GROUPS, grad_step, 0)
    dcs[...] = acc[...].T.reshape(GROUPS, SUB, CODES)

    s_c = block(16)
    for a in range(4):
        for b in range(4):
            if (a, b) != (0, 0):
                other = ((y + a) % 4) * 4 + (z + b) % 4
                push(dcs.at[other], dcr.at[me], s_c + ((4 - a) % 4) * 4 + (4 - b) % 4, dev_yz(a, b))
    dcr[me] = dcs[me]
    for a in range(4):
        for b in range(4):
            if (a, b) != (0, 0):
                arrive(dcr.at[((y + a) % 4) * 4 + (z + b) % 4], s_c + a * 4 + b)
    piece[...] = jnp.sum(dcr[...], axis=0)

    s_x = block(8)
    dbuf[me, mine] = piece[...]
    for step in range(4):
        for other in range(2):
            if (step, other) != (0, 0):
                who = core if other == 0 else 1 - core
                push(piece, dbuf.at[me, mine], s_x + ((4 - step) % 4) * 2 + other, dev_x(step, who))
    for step in range(4):
        for other in range(2):
            if (step, other) != (0, 0):
                s = r_slot(step) if other == 0 else r_sib(step)
                arrive(dbuf.at[me, s], s_x + step * 2 + other)

    def d_piece(s, h, part):
        if part is None:
            return dbuf.at[s, pl.ds(4 * h, 3), :, :]
        return dbuf.at[s, pl.ds(4 * h, 3), :, pl.ds(128 * part, 128)]

    dw = gather_plane(lambda h: d_piece(me, h, None), d_piece, block(64))
    for wave in dw:
        wave()
    for t in range(6):
        for p in range(PLANE):
            out_ref[t * TILE + p * SUB:t * TILE + (p + 1) * SUB, :] = dbuf[p, t + (t // 3)]

    arrive(divb.at[1 - xl], s_d)
    for k in range(4):
        for h in range(2):
            div_ref[4 * k + 2 * h:4 * k + 2 * h + 2, :] = divb[h, 2 * k:2 * k + 2, :]

    for copy in sends:
        copy.wait_send()


def local(passages, queries, codebook):
    vmem = pl.BlockSpec(memory_space=pltpu.VMEM)
    grad, divergence = pl.pallas_call(
        kernel,
        out_shape=(
            jax.ShapeDtypeStruct((D, CODES), F32),
            jax.ShapeDtypeStruct((16, 128), F32),
        ),
        in_specs=[vmem] * 3,
        out_specs=(vmem, vmem),
        scratch_shapes=[
            pltpu.VMEM((PLANE, QB, D), BF16),
            pltpu.VMEM((2, PB, D), BF16),
            pltpu.VMEM((8, ROWS, TILE), BF16),
            pltpu.VMEM((CODES, 4 * TILE), BF16),
            pltpu.VMEM((CODES, 4 * TILE), BF16),
            pltpu.VMEM((GROUPS, 32, CODES), BF16),
            pltpu.VMEM((CODES, TILE), F32),
            pltpu.VMEM((GROUPS, SUB, ROWS), F32),
            pltpu.VMEM((GROUPS, CODES, ROWS), BF16),
            pltpu.VMEM((GROUPS, CODES, ROWS), BF16),
            pltpu.VMEM((4, ROWS, 256), F32),
            pltpu.VMEM((4, ROWS, 256), F32),
            pltpu.VMEM((4, ROWS, 256), F32),
            pltpu.VMEM((16, 128), F32),
            pltpu.VMEM((PLANE, 24, 128), F32),
            pltpu.VMEM((4, ROWS, TILE), F32),
            pltpu.VMEM((3, ROWS, TILE), F32),
            pltpu.VMEM((3, ROWS, TILE), F32),
            pltpu.VMEM((2, 128, TILE), F32),
            pltpu.VMEM((2, 128, TILE), F32),
            pltpu.VMEM((2, ROWS, TILE), F32),
            pltpu.VMEM((2, ROWS, TILE), F32),
            pltpu.VMEM((CODES, TILE), F32),
            pltpu.VMEM((PLANE, SUB, CODES), F32),
            pltpu.VMEM((PLANE, SUB, CODES), F32),
            pltpu.VMEM((SUB, CODES), F32),
            pltpu.VMEM((PLANE, 8, SUB, CODES), F32),
            pltpu.VMEM((2, 8, 128), F32),
            pltpu.SemaphoreType.DMA((N_SEM,)),
            pltpu.SemaphoreType.DMA((192,)),
        ],
        compiler_params=pltpu.CompilerParams(
            collective_id=0, has_side_effects=True, vmem_limit_bytes=60 * 1024 * 1024
        ),
    )(passages, queries, codebook.reshape(D, CODES))
    return divergence.reshape(2048), grad.reshape(96, SUB, CODES)


def solution(mesh):
    placed = (P("corpus", None), P(("query", "corpus"), None), P())
    return jax.shard_map(
        local, mesh=mesh, in_specs=placed, out_specs=(P("query"), P()), check_vma=False
    )
```

time: 736 us -> 87.7 us (0.12)
  the two profiles are of different devices: /device:TPU:1 before, /device:TPU:0 now
where the time goes in v1:
time: 87.7 us; the launch traced here: 87.5 us
  Pallas kernels  83.5 us (95%)
  local copies, waits for them, and re-layouts  3.36 us (4%)
    pallas_call x1, Pallas kernels, local(): pl.pallas_call(kernel, out_shape=(jax.ShapeDtypeStruct((D, CODES), F32),...  83.5 us
    unnamed x2, local copies, waits for them, and re-layouts  3.36 us

profile of v1, /device:TPU:0, one launch (start us, length us, event | category | flops | bytes accessed | tf_op | source)
XLA Modules:
  0.0 87.5 jit_solution(911074428768187650)
XLA Ops:
  0.6 83.5 %shard_map.50 = (f32[768,256]{1,0:T(8,128)}, f32[16,128]{1,0:T(8,128)}) custom-call(bf16[128,768]{1,0:T(8,128)(2,1)} %p_ref.1, bf16[64,768]{1,0:T(8,128)(2,1)} %q_ref.1, f32[768,256]{1,0:T(8,128)} %bitcast.4), custom_call_target="tpu_custom_call" | custom-call | tf_op jit(solution)/shard_map/pallas_call | solution.py:442
  84.2 1.3 %copy.7 = f32[2048]{0:T(1024)} copy(f32[2048]{0:T(1024)} %bitcast.5) | data formatting | bytes 16384
  85.5 2.1 %copy.8 = f32[96,8,256]{2,1,0:T(8,128)} copy(f32[96,8,256]{2,1,0:T(8,128)} %bitcast.3) | data formatting | bytes 1572864

commit v2 on v1

--- a/solution.py
+++ b/solution.py
@@ -23,7 +23,8 @@
 GROUPS = 16
 ROWS = 256
 QN = 1024
-N_SEM = 136
+N_SEM = 160
+FAR_FIRST = [(2, 2), (2, 1), (2, 3), (1, 2), (3, 2), (1, 1), (1, 3), (3, 1), (3, 3), (2, 0), (0, 2), (1, 0), (3, 0), (0, 1), (0, 3)]
 
 
 def split3(value):
@@ -49,8 +50,8 @@
     out_ref, div_ref,
     qbuf, pbuf, rbuf,
     lhs_f, lhs_b, cp3, ct, rt, a1b, a2b,
-    tbuf, ebt, ebs, mloc, stat,
-    gown, gsib, gsrc, rs1, rs1s, rs2, rs2s,
+    tbuf, ebt, ebs, mloc, stat_t, stat,
+    gown, gsib, gsrc, rs1, rs2, rs2s,
     acc, dcs, dcr, piece, dbuf, divb,
     send_sem, recv_sem,
 ):
@@ -76,19 +77,25 @@
     sends = []
     count = [0]
 
-    def push(src, dst, index, device):
+    def guarded(cond, action):
+        if cond is None:
+            action()
+        else:
+            pl.when(cond)(action)
+
+    def push(src, dst, index, device, cond=None):
         copy = pltpu.make_async_remote_copy(
             src_ref=src, dst_ref=dst, send_sem=send_sem.at[len(sends)],
             recv_sem=recv_sem.at[index], device_id=device, device_id_type=MESH,
         )
-        copy.start()
-        sends.append(copy)
-
-    def arrive(dst, index):
-        pltpu.make_async_remote_copy(
+        guarded(cond, copy.start)
+        sends.append((copy, cond))
+
+    def arrive(dst, index, cond=None):
+        guarded(cond, pltpu.make_async_remote_copy(
             src_ref=dst, dst_ref=dst, send_sem=send_sem.at[0],
             recv_sem=recv_sem.at[index], device_id=sibling, device_id_type=MESH,
-        ).wait_recv()
+        ).wait_recv)
 
     def block(n):
         first = count[0]
@@ -129,16 +136,17 @@
             arrive(piece_of(slot(dy, dz), h, part), sem(dy, dz, h, part))
 
         def wave0():
-            for first in (True, False):
-                for h in range(2):
-                    for step in (1, 3):
-                        send(h, 0, 0, None, first, step)
+            for h in range(2):
+                for step in (1, 3, 2):
+                    send(h, 0, 0, None, True, step)
+            for h in range(2):
+                for step in (1, 3):
+                    send(h, 0, 0, None, False, step)
 
         def wave1():
             for h in range(2):
-                for a, part, step in ((3, 0, 1), (1, 1, 3)):
+                for a in (3, 1):
                     wait(h, a, 0, None)
-                    send(h, a, 0, part, True, step)
                     send(h, a, 0, None, False, 1)
                     send(h, a, 0, None, False, 3)
             for h in range(2):
@@ -148,10 +156,9 @@
 
         def wave2():
             for h in range(2):
-                wait(h, 2, 0, 0)
-                wait(h, 2, 0, 1)
-                send(h, 2, 0, None, False, 1)
-                send(h, 2, 0, None, False, 3)
+                wait(h, 2, 0, None)
+                for step in (2, 1, 3):
+                    send(h, 2, 0, None, False, step)
             for h in range(2):
                 for a in (3, 1):
                     for b, part, step in ((3, 0, 1), (1, 1, 3)):
@@ -160,17 +167,13 @@
 
         def wave3():
             for h in range(2):
-                for b, part, step in ((3, 0, 1), (1, 1, 3)):
-                    wait(h, 2, b, None)
-                    send(h, 2, b, part, False, step)
-
-        def wave4():
-            for h in range(2):
-                for a in (0, 1, 3, 2):
+                for a in (0, 1, 3):
                     wait(h, a, 2, 0)
                     wait(h, a, 2, 1)
-
-        return wave0, wave1, wave2, wave3, wave4
+                for b in (1, 3, 2):
+                    wait(h, 2, b, None)
+
+        return wave0, wave1, wave2, wave3
 
     def q_piece(s, h, part):
         if part is None:
@@ -245,21 +248,18 @@
     def r_sib(step):
         return (1 - core) * 4 + (u + 2 + step) % 4
 
-    def r_half(s, part):
-        return rbuf.at[s, pl.ds(128 * part, 128), :]
-
     s_r = block(4)
-    s_rs = block(5)
-    push(rbuf.at[mine], rbuf.at[mine], s_r + 0, right)
-    push(rbuf.at[mine], rbuf.at[mine], s_r + 1, left)
-    push(rbuf.at[mine], rbuf.at[mine], s_rs + 0, sibling)
+    s_rs = block(4)
+    owner = u != 3
+    for step in (2, 1, 3):
+        push(rbuf.at[mine], rbuf.at[mine], s_r + 4 - step, dev_x(step), owner)
+    push(rbuf.at[mine], rbuf.at[mine], s_rs, sibling, owner)
+    for step in (1, 3, 2):
+        s = r_slot(step)
+        real = (u + step) % 4 != 3
+        arrive(rbuf.at[s], s_r + step, real)
+        push(rbuf.at[s], rbuf.at[s], s_rs + step, sibling, real)
     qw[3]()
-    for step, sem_i, part, far in ((3, 0, 0, right), (1, 1, 1, left)):
-        s = r_slot(step)
-        arrive(rbuf.at[s], s_r + sem_i)
-        push(r_half(s, part), r_half(s, part), s_r + 2 + part, far)
-        push(rbuf.at[s], rbuf.at[s], s_rs + 1 + sem_i, sibling)
-    qw[4]()
 
     p_all = pbuf[...].reshape(ROWS, D)
     scale = float(D) ** (-0.5)
@@ -273,18 +273,20 @@
         lt = m_t + jnp.log(jnp.sum(e_t, axis=0, keepdims=True))
         for k in range(2):
             mloc[2 * n + k:2 * n + k + 1, :] = m_t[:, 128 * k:128 * k + 128]
-            stat[me, 2 * n + k:2 * n + k + 1, :] = lt[:, 128 * k:128 * k + 128]
-        if n == 0:
-            far_slot = r_slot(2)
-            for part in range(2):
-                arrive(r_half(far_slot, part), s_r + 2 + part)
-                push(r_half(far_slot, part), r_half(far_slot, part), s_rs + 3 + part, sibling)
-
-    arrive(rbuf.at[r_sib(0)], s_rs + 0)
-    arrive(rbuf.at[r_sib(3)], s_rs + 1)
-    arrive(rbuf.at[r_sib(1)], s_rs + 2)
-    for part in range(2):
-        arrive(r_half(r_sib(2), part), s_rs + 3 + part)
+            stat_t[me, 2 * n + k:2 * n + k + 1, :] = lt[:, 128 * k:128 * k + 128]
+
+    def plane_send(buf, base):
+        for a, b in FAR_FIRST:
+            push(buf.at[me], buf.at[me], base + ((4 - a) % 4) * 4 + (4 - b) % 4, dev_yz(a, b))
+
+    def plane_wait(buf, base):
+        for a, b in FAR_FIRST:
+            arrive(buf.at[((y + a) % 4) * 4 + (z + b) % 4], base + a * 4 + b)
+
+    s_ta = block(16)
+    plane_send(stat_t, s_ta)
+    for step in (0, 1, 3, 2):
+        arrive(rbuf.at[r_sib(step)], s_rs + step, (u + 2 + step) % 4 != 3)
 
     r_all = jnp.concatenate([rbuf[k] for k in (0, 1, 2, 4, 5, 6)], axis=1)
     for n in range(4):
@@ -300,21 +302,15 @@
         for k in range(2):
             r = 2 * n + k
             mloc[8 + r:9 + r, :] = m_s[:, 128 * k:128 * k + 128]
-            stat[me, 8 + r:9 + r, :] = ls[:, 128 * k:128 * k + 128]
-            stat[me, 16 + r:17 + r, :] = cross[:, 128 * k:128 * k + 128]
+            stat[me, r:r + 1, :] = ls[:, 128 * k:128 * k + 128]
+            stat[me, 8 + r:9 + r, :] = cross[:, 128 * k:128 * k + 128]
 
     s_st = block(16)
-    for a in range(4):
-        for b in range(4):
-            if (a, b) != (0, 0):
-                push(stat.at[me], stat.at[me], s_st + ((4 - a) % 4) * 4 + (4 - b) % 4, dev_yz(a, b))
-    for a in range(4):
-        for b in range(4):
-            if (a, b) != (0, 0):
-                arrive(stat.at[((y + a) % 4) * 4 + (z + b) % 4], s_st + a * 4 + b)
-
-    st = stat[...]
-    lt, ls, cx = st[:, 0:8], st[:, 8:16], st[:, 16:24]
+    plane_send(stat, s_st)
+    plane_wait(stat_t, s_ta)
+    lt = stat_t[...]
+    plane_wait(stat, s_st)
+    ls, cx = stat[:, 0:8], stat[:, 8:16]
     top_t = jnp.max(lt, axis=0)
     top_s = jnp.max(ls, axis=0)
     big_t = top_t + jnp.log(jnp.sum(jnp.exp(lt - top_t[None]), axis=0))
@@ -336,35 +332,49 @@
             grads.append((diff * weight).astype(BF16))
     grad_scores = jnp.concatenate(grads, axis=1)
 
-    def partial(group, dest):
-        for k in range(3):
-            at = pl.multiple_of(group * 384 + 128 * k, 128)
-            qcol = qbuf[:, :, pl.ds(at, 128)].reshape(QN, 128)
-            dest[k] = dot(grad_scores, qcol, NN)
-
-    partial(1 - core, gsrc)
-    s_g = block(1)
-    push(gsrc, gsib, s_g, sibling)
-    partial(core, gown)
-    gown[3] = jnp.zeros((ROWS, TILE), F32)
-    arrive(gsib, s_g)
-    gown[0:3] = gown[0:3] + gsib[...]
+    def partial(group, d):
+        at = pl.multiple_of(group * 384 + jnp.minimum(d, 2) * TILE, TILE)
+        return dot(grad_scores, qbuf[:, :, pl.ds(at, TILE)].reshape(QN, TILE), NN)
+
+    s_g = block(4)
+    order = (2, 1, 3, 0)
+    for k, step in enumerate(order):
+        gsrc[k] = partial(1 - core, (u + 2 + step) % 4)
+        push(gsrc.at[k], gsib.at[k], s_g + k, sibling)
+    for k, step in enumerate(order):
+        gown[k] = partial(core, (u + step) % 4)
 
     s_1 = block(2)
-    s_2 = block(2)
-    far = (u + 2) % 4
+    s_2 = block(4)
+
+    def half(n):
+        return pl.ds(128 * n, 128)
+
+    far_ok = (u + 2) % 4 != 3
+    arrive(gsib.at[0], s_g)
+    gown[0] = gown[0] + gsib[0]
     for part, to in ((0, right), (1, left)):
-        push(gown.at[far, pl.ds(128 * part, 128), :], rs1.at[part], s_1 + part, to)
+        push(gown.at[0, half(part), :], rs1.at[part], s_1 + part, to, far_ok)
     for part, to, step in ((0, right, 1), (1, left, 3)):
-        d = (u + step) % 4
-        arrive(rs1.at[part], s_1 + part)
-        keep, add = (128, 0) if part == 0 else (0, 128)
-        rs2s[part, pl.ds(keep, 128), :] = gown[d, pl.ds(keep, 128), :]
-        rs2s[part, pl.ds(add, 128), :] = gown[d, pl.ds(add, 128), :] + rs1[part]
-        push(rs2s.at[part], rs2.at[part], s_2 + part, to)
-    arrive(rs2.at[0], s_2)
-    arrive(rs2.at[1], s_2 + 1)
-    g = gown[u] + rs2[0] + rs2[1]
+        k = 1 + part
+        arrive(gsib.at[k], s_g + k)
+        gown[k] = gown[k] + gsib[k]
+        push(
+            gown.at[k, half(1 - part), :], rs2.at[part, half(1 - part), :],
+            s_2 + 2 * part, to, (u + step) % 4 != 3,
+        )
+    arrive(gsib.at[3], s_g + 3)
+    gown[3] = gown[3] + gsib[3]
+    for part, to, step in ((0, right, 1), (1, left, 3)):
+        k = 1 + part
+        ok = (u + step) % 4 != 3
+        arrive(rs1.at[part], s_1 + part, ok)
+        rs2s[part] = gown[k, half(part), :] + rs1[part]
+        push(rs2s.at[part], rs2.at[part, half(part), :], s_2 + 2 * part + 1, to, ok)
+    for part in range(2):
+        arrive(rs2.at[part, half(1 - part), :], s_2 + 2 * part, owner)
+        arrive(rs2.at[part, half(part), :], s_2 + 2 * part + 1, owner)
+    g = gown[3] + rs2[0] + rs2[1]
 
     g1, g2 = split2(g)
     gt = g.T
@@ -391,39 +401,34 @@
     dcs[...] = acc[...].T.reshape(GROUPS, SUB, CODES)
 
     s_c = block(16)
-    for a in range(4):
-        for b in range(4):
-            if (a, b) != (0, 0):
-                other = ((y + a) % 4) * 4 + (z + b) % 4
-                push(dcs.at[other], dcr.at[me], s_c + ((4 - a) % 4) * 4 + (4 - b) % 4, dev_yz(a, b))
+    for a, b in FAR_FIRST:
+        other = ((y + a) % 4) * 4 + (z + b) % 4
+        push(dcs.at[other], dcr.at[me], s_c + ((4 - a) % 4) * 4 + (4 - b) % 4, dev_yz(a, b))
     dcr[me] = dcs[me]
-    for a in range(4):
-        for b in range(4):
-            if (a, b) != (0, 0):
-                arrive(dcr.at[((y + a) % 4) * 4 + (z + b) % 4], s_c + a * 4 + b)
+    plane_wait(dcr, s_c)
     piece[...] = jnp.sum(dcr[...], axis=0)
 
-    s_x = block(8)
+    s_x = block(4)
     dbuf[me, mine] = piece[...]
-    for step in range(4):
-        for other in range(2):
-            if (step, other) != (0, 0):
-                who = core if other == 0 else 1 - core
-                push(piece, dbuf.at[me, mine], s_x + ((4 - step) % 4) * 2 + other, dev_x(step, who))
-    for step in range(4):
-        for other in range(2):
-            if (step, other) != (0, 0):
-                s = r_slot(step) if other == 0 else r_sib(step)
-                arrive(dbuf.at[me, s], s_x + step * 2 + other)
-
-    def d_piece(s, h, part):
-        if part is None:
-            return dbuf.at[s, pl.ds(4 * h, 3), :, :]
-        return dbuf.at[s, pl.ds(4 * h, 3), :, pl.ds(128 * part, 128)]
-
-    dw = gather_plane(lambda h: d_piece(me, h, None), d_piece, block(64))
-    for wave in dw:
-        wave()
+    for step in (2, 1, 3):
+        push(piece, dbuf.at[me, mine], s_x + 4 - step, dev_x(step), owner)
+    for step in (1, 3, 2):
+        arrive(dbuf.at[me, r_slot(step)], s_x + step, (u + step) % 4 != 3)
+
+    def trio(s, c):
+        return dbuf.at[s, pl.ds(4 * c, 3), :, :]
+
+    s_f = block(16)
+    s_fs = block(16)
+    for a, b in FAR_FIRST:
+        push(trio(me, core), trio(me, core), s_f + ((4 - a) % 4) * 4 + (4 - b) % 4, dev_yz(a, b))
+    push(trio(me, core), trio(me, core), s_fs, sibling)
+    for a, b in FAR_FIRST[::-1]:
+        s = ((y + a) % 4) * 4 + (z + b) % 4
+        arrive(trio(s, core), s_f + a * 4 + b)
+        push(trio(s, core), trio(s, core), s_fs + a * 4 + b, sibling)
+    for a, b in [(0, 0)] + FAR_FIRST[::-1]:
+        arrive(trio(((y + a) % 4) * 4 + (z + b) % 4, 1 - core), s_fs + a * 4 + b)
     for t in range(6):
         for p in range(PLANE):
             out_ref[t * TILE + p * SUB:t * TILE + (p + 1) * SUB, :] = dbuf[p, t + (t // 3)]
@@ -433,8 +438,8 @@
         for h in range(2):
             div_ref[4 * k + 2 * h:4 * k + 2 * h + 2, :] = divb[h, 2 * k:2 * k + 2, :]
 
-    for copy in sends:
-        copy.wait_send()
+    for copy, cond in sends:
+        guarded(cond, copy.wait_send)
 
 
 def local(passages, queries, codebook):
@@ -462,14 +467,14 @@
             pltpu.VMEM((4, ROWS, 256), F32),
             pltpu.VMEM((4, ROWS, 256), F32),
             pltpu.VMEM((16, 128), F32),
-            pltpu.VMEM((PLANE, 24, 128), F32),
+            pltpu.VMEM((PLANE, 8, 128), F32),
+            pltpu.VMEM((PLANE, 16, 128), F32),
             pltpu.VMEM((4, ROWS, TILE), F32),
-            pltpu.VMEM((3, ROWS, TILE), F32),
-            pltpu.VMEM((3, ROWS, TILE), F32),
-            pltpu.VMEM((2, 128, TILE), F32),
+            pltpu.VMEM((4, ROWS, TILE), F32),
+            pltpu.VMEM((4, ROWS, TILE), F32),
             pltpu.VMEM((2, 128, TILE), F32),
             pltpu.VMEM((2, ROWS, TILE), F32),
-            pltpu.VMEM((2, ROWS, TILE), F32),
+            pltpu.VMEM((2, 128, TILE), F32),
             pltpu.VMEM((CODES, TILE), F32),
             pltpu.VMEM((PLANE, SUB, CODES), F32),
             pltpu.VMEM((PLANE, SUB, CODES), F32),
@@ -477,7 +482,7 @@
             pltpu.VMEM((PLANE, 8, SUB, CODES), F32),
             pltpu.VMEM((2, 8, 128), F32),
             pltpu.SemaphoreType.DMA((N_SEM,)),
-            pltpu.SemaphoreType.DMA((192,)),
+            pltpu.SemaphoreType.DMA((200,)),
         ],
         compiler_params=pltpu.CompilerParams(
             collective_id=0, has_side_effects=True, vmem_limit_bytes=60 * 1024 * 1024

time: 87.7 us -> 78.1 us (0.89)
  the two profiles are of different devices: /device:TPU:0 before, /device:TPU:1 now
where the time goes in v2:
time: 78.1 us; the launch traced here: 77.9 us
  Pallas kernels  73.9 us (95%)
  local copies, waits for them, and re-layouts  3.36 us (4%)
    pallas_call x1, Pallas kernels, local(): pl.pallas_call(kernel, out_shape=(jax.ShapeDtypeStruct((D, CODES), F32),...  73.9 us
    unnamed x2, local copies, waits for them, and re-layouts  3.36 us

profile of v2, /device:TPU:1, one launch (start us, length us, event | category | flops | bytes accessed | tf_op | source)
XLA Modules:
  0.0 77.9 jit_solution(15863385550946358532)
XLA Ops:
  0.6 73.9 %shard_map.50 = (f32[768,256]{1,0:T(8,128)}, f32[16,128]{1,0:T(8,128)}) custom-call(bf16[128,768]{1,0:T(8,128)(2,1)} %p_ref.1, bf16[64,768]{1,0:T(8,128)(2,1)} %q_ref.1, f32[768,256]{1,0:T(8,128)} %bitcast.4), custom_call_target="tpu_custom_call" | custom-call | tf_op jit(solution)/shard_map/pallas_call | solution.py:447
  74.6 1.3 %copy.7 = f32[2048]{0:T(1024)} copy(f32[2048]{0:T(1024)} %bitcast.5) | data formatting | bytes 16384
  75.8 2.1 %copy.8 = f32[96,8,256]{2,1,0:T(8,128)} copy(f32[96,8,256]{2,1,0:T(8,128)} %bitcast.3) | data formatting | bytes 1572864

commit v3 on v2

--- a/solution.py
+++ b/solution.py
@@ -23,6 +23,7 @@
 GROUPS = 16
 ROWS = 256
 QN = 1024
+BEFORE = 3
 N_SEM = 160
 FAR_FIRST = [(2, 2), (2, 1), (2, 3), (1, 2), (3, 2), (1, 1), (1, 3), (3, 1), (3, 3), (2, 0), (0, 2), (1, 0), (3, 0), (0, 1), (0, 3)]
 
@@ -49,10 +50,10 @@
     p_ref, q_ref, cb_ref,
     out_ref, div_ref,
     qbuf, pbuf, rbuf,
-    lhs_f, lhs_b, cp3, ct, rt, a1b, a2b,
+    xtb, xpack, lhs_f, cp3, rt, inv, a1b, a2b,
     tbuf, ebt, ebs, mloc, stat_t, stat,
     gown, gsib, gsrc, rs1, rs2, rs2s,
-    acc, dcs, dcr, piece, dbuf, divb,
+    gl, ts, xlt, gpack, dcs, dcr, piece, dbuf, divb,
     send_sem, recv_sem,
 ):
     qi = lax.axis_index("query")
@@ -112,6 +113,69 @@
     qbuf[me] = q_ref[...]
     pbuf[xl] = p_ref[...]
 
+    def tile_col(u_):
+        return pl.multiple_of((3 * core + jnp.minimum(u_, 2)) * TILE, TILE)
+
+    col = tile_col(u)
+    cb = cb_ref[pl.ds(col, TILE), :]
+    grouped = cb.reshape(GROUPS, SUB, CODES)
+    bias = -0.5 * jnp.sum(grouped * grouped, axis=1, keepdims=True)
+    b_parts = [jnp.broadcast_to(b.astype(F32), grouped.shape) for b in split3(bias)]
+    row = lax.broadcasted_iota(jnp.int32, grouped.shape, 1)
+    extra = jnp.where(row == 3, 1.0, 0.0)
+    for k in range(3):
+        extra = jnp.where(row == k, b_parts[k], extra)
+    c_parts = [c.astype(F32).reshape(GROUPS, SUB, CODES) for c in split3(cb)]
+    packed = jnp.concatenate(c_parts + [extra], axis=1)
+    cp3[...] = packed.reshape(8, 64, CODES).astype(BF16)
+    for g in range(4):
+        lhs_f[g] = packed[4 * g:4 * g + 4].reshape(TILE, CODES).T.astype(BF16)
+
+    lane = lax.broadcasted_iota(jnp.int32, (TILE, 4 * TILE), 1)
+    source = lax.broadcasted_iota(jnp.int32, (TILE, 4 * TILE), 0)
+    inner_lane = lane % 32
+    select = jnp.where(
+        (source == (lane // 32) * SUB + lane % SUB) & (inner_lane < 24), 1.0, 0.0
+    ).astype(BF16)
+    tail_ones = jnp.where(
+        (inner_lane[0:1] >= 24) & (inner_lane[0:1] < 27), 1.0, 0.0
+    )
+    pack_lane = lax.broadcasted_iota(jnp.int32, (1, TILE), 1) // 32
+
+    def pack_mask(j):
+        return jnp.where(pack_lane == j, 1.0, 0.0).astype(BF16)
+
+    def pack_rows(h):
+        packs = (dot(xtb[h], select, NN) + tail_ones).astype(BF16)
+        for g in range(4):
+            xpack[g] = packs[:, TILE * g:TILE * g + TILE]
+
+    def assign_step(h):
+        lanes = pl.ds(pl.multiple_of(h * 128, 128), 128)
+
+        def step(v, carry):
+            g, j = v // 2, 2 * (v % 2)
+            xp = xpack[g]
+            rhs = jnp.concatenate([xp * pack_mask(j), xp * pack_mask(j + 1)], axis=0)
+            logits = dot(lhs_f[g], rhs, NT)
+            e1, e2 = split2(jnp.exp(logits - jnp.max(logits, axis=0, keepdims=True)))
+            got = dot(cp3[v], e1, NN) + dot(cp3[v], e2, NN)
+            for k in range(2):
+                i = 2 * v + k
+                half_lanes = slice(128 * k, 128 * k + 128)
+                a1b[i, :, lanes] = e1[:, half_lanes]
+                a2b[i, :, lanes] = e2[:, half_lanes]
+                part = got[32 * k:32 * k + 32, half_lanes]
+                scale_i = 1.0 / part[27:28]
+                inv[i, :, lanes] = scale_i
+                rt[i, :, lanes] = (part[0:8] + part[8:16] + part[16:24]) * scale_i
+            return carry
+
+        return step
+
+    xtb[xl] = p_ref[:, pl.ds(col, TILE)]
+    pack_rows(xl)
+    lax.fori_loop(0, BEFORE, assign_step(xl), 0)
     pl.semaphore_wait(barrier, len(peers))
 
     def gather_plane(own, piece_of, base):
@@ -181,63 +245,21 @@
         return qbuf.at[s, pl.ds(32 * h + 16 * part, 16), :]
 
     qw = gather_plane(lambda h: q_ref.at[pl.ds(32 * h, 32), :], q_piece, block(64))
-    s_p = block(1)
+    s_p = block(2)
     x_to = (x + 3 + 2 * core) % 4
-    push(p_ref, pbuf.at[xl], s_p, dev(x_to, y, z, core))
+    p_to = dev(x_to, y, z, core)
+    col_to = tile_col((x_to + 4 - 2 * core) % 4)
+    push(p_ref.at[:, pl.ds(col_to, TILE)], xtb.at[xl], s_p, p_to)
     qw[0]()
-
-    tile = 3 * core + jnp.minimum(u, 2)
-    col = pl.multiple_of(tile * TILE, TILE)
-    cb = cb_ref[pl.ds(col, TILE), :]
-    grouped = cb.reshape(GROUPS, SUB, CODES)
-    bias = -0.5 * jnp.sum(grouped * grouped, axis=1)
-    c_parts = split3(cb)
-    c32 = [c.astype(F32).reshape(GROUPS, SUB, CODES) for c in c_parts]
-    cp3[...] = jnp.concatenate(c32 + [jnp.zeros((GROUPS, SUB, CODES), F32)], axis=1).astype(BF16)
-    cbt = cb.T
-    ct[...] = cbt
-    t1, t2, t3 = split3(cbt)
-
-    def stack_rows(parts, width):
-        rows = [p.astype(F32) for p in parts]
-        rows.append(jnp.zeros((TILE - len(parts) * GROUPS, width), F32))
-        return jnp.concatenate(rows, axis=0).T.astype(BF16)
-
-    lane = lax.broadcasted_iota(jnp.int32, (1, 4 * TILE), 1)
-    in_tile = lane % TILE
-    group_id = jnp.where(
-        lane < 3 * TILE, in_tile // SUB, jnp.where(in_tile < 3 * GROUPS, in_tile % GROUPS, -1)
-    )
-    ones48 = jnp.where(
-        lax.broadcasted_iota(jnp.int32, (CODES, TILE), 1) < 3 * GROUPS, 1.0, 0.0
-    ).astype(BF16)
-    lhs_f[...] = jnp.concatenate([t1, t2, t3, stack_rows(split3(bias), CODES)], axis=1)
-    lhs_b[...] = jnp.concatenate([t1, t1, t2, ones48], axis=1)
-
+    push(p_ref, pbuf.at[xl], s_p + 1, p_to)
+
+    lax.fori_loop(BEFORE, 8, assign_step(xl), 0)
     qw[1]()
-    arrive(pbuf.at[1 - xl], s_p)
-
-    xt = jnp.concatenate([pbuf[0, :, pl.ds(col, TILE)], pbuf[1, :, pl.ds(col, TILE)]], axis=0)
-    rhs_f = jnp.concatenate([xt, xt, xt, ones48], axis=1)
-
-    def group_mask(i):
-        return jnp.where(group_id == i, 1.0, 0.0).astype(BF16)
-
-    def assign_step(i, carry):
-        logits = dot(lhs_f[...] * group_mask(i), rhs_f, NT)
-        top = jnp.max(logits, axis=0, keepdims=True)
-        e = jnp.exp(logits - top)
-        w = e * (1.0 / jnp.sum(e, axis=0, keepdims=True))
-        w1, w2 = split2(w)
-        a1b[i] = w1
-        a2b[i] = w2
-        got = dot(cp3[i], w1, NN) + dot(cp3[i], w2, NN)
-        rt[i] = got[0:8] + got[8:16] + got[16:24]
-        return carry
-
-    lax.fori_loop(0, 8, assign_step, 0)
+    arrive(xtb.at[1 - xl], s_p)
+    pack_rows(1 - xl)
+    lax.fori_loop(0, 4, assign_step(1 - xl), 0)
     qw[2]()
-    lax.fori_loop(8, 16, assign_step, 0)
+    lax.fori_loop(4, 8, assign_step(1 - xl), 0)
 
     mine = core * 4 + u
     rbuf[mine] = rt[...].reshape(TILE, ROWS).T.astype(BF16)
@@ -260,6 +282,7 @@
         arrive(rbuf.at[s], s_r + step, real)
         push(rbuf.at[s], rbuf.at[s], s_rs + step, sibling, real)
     qw[3]()
+    arrive(pbuf.at[1 - xl], s_p + 1)
 
     p_all = pbuf[...].reshape(ROWS, D)
     scale = float(D) ** (-0.5)
@@ -376,36 +399,61 @@
         arrive(rs2.at[part, half(part), :], s_2 + 2 * part + 1, owner)
     g = gown[3] + rs2[0] + rs2[1]
 
-    g1, g2 = split2(g)
-    gt = g.T
-    inner = jnp.sum((gt * rt[...].reshape(TILE, ROWS)).reshape(GROUPS, SUB, ROWS), axis=1)
-    rhs_b = jnp.concatenate([g1, g2, g1, stack_rows(split3(-inner), ROWS)], axis=1)
-    g12 = jnp.concatenate([g1, g2], axis=1)
-    xo = jnp.concatenate([xt, jnp.full((ROWS, TILE), 1.0, BF16)], axis=1)
-    lane_group = lax.broadcasted_iota(jnp.int32, (1, TILE), 1) // SUB
-
-    def grad_step(i, carry):
-        diff = dot(lhs_b[...] * group_mask(i), rhs_b, NT)
-        w1 = a1b[i]
-        w2 = a2b[i]
-        d1, d2 = split2((w1.astype(F32) + w2.astype(F32)) * diff)
-        o1 = dot(w1, g12, NN)
-        o2 = dot(w2, g1, NN)
-        o3 = dot(d1, xo, NN) + dot(d2, xo, NN)
-        val = o1[:, :TILE] + o1[:, TILE:] + o2 + o3[:, :TILE] - ct[...] * o3[:, TILE:]
-        acc[...] = jnp.where(lane_group == i, val, acc[...])
+    xt = xtb[...].reshape(ROWS, TILE)
+    gt = (g.T).reshape(GROUPS, SUB, ROWS) * inv[...]
+    g1t, g2t = split2(gt)
+    gl[...] = jnp.concatenate([g1t.astype(F32), g2t.astype(F32)], axis=1).astype(BF16)
+    ts[...] = jnp.sum(gt * rt[...], axis=1, keepdims=True)
+    xlt[...] = jnp.concatenate(
+        [xt.astype(F32).T.reshape(GROUPS, SUB, ROWS), jnp.full((GROUPS, SUB, ROWS), 1.0, F32)], axis=1
+    ).astype(BF16)
+    back = gt.reshape(TILE, ROWS).T
+    for n, part in enumerate(split2(back)):
+        packs = dot(part, select, NN).astype(BF16)
+        for k in range(4):
+            gpack[k, :, TILE * n:TILE * n + TILE] = packs[:, TILE * k:TILE * k + TILE]
+
+    s_c = block(16)
+    first_c = len(sends)
+    sends.extend([None] * 15)
+
+    def piece_copy(n):
+        other = (me + 1 + n) % 16
+        return pltpu.make_async_remote_copy(
+            src_ref=dcs.at[other], dst_ref=dcr.at[me], send_sem=send_sem.at[first_c + n],
+            recv_sem=recv_sem.at[s_c + me], device_id=dev(x, other // 4, other % 4, core),
+            device_id_type=MESH,
+        )
+
+    def grad_step(n, carry):
+        i = (me + 1 + n) % 16
+
+        @pl.when(n > 0)
+        def _():
+            piece_copy(n - 1).start()
+
+        p, j = i // 4, i % 4
+        lp = lhs_f[p]
+        mask = pack_mask(j)
+        diff = dot(
+            jnp.concatenate([lp, lp], axis=1),
+            gpack[p] * jnp.concatenate([mask, mask], axis=1), NT,
+        )
+        e1 = a1b[i]
+        e2 = a2b[i]
+        d1, d2 = split2((e1.astype(F32) + e2.astype(F32)) * (diff - ts[i]))
+        ow = dot(gl[i], e1, NT) + dot(gl[i], e2, NT)
+        od = dot(xlt[i], d1, NT) + dot(xlt[i], d2, NT)
+        code = cb_ref[pl.ds(pl.multiple_of(col + SUB * i, SUB), SUB), :]
+        dcs[i] = ow[0:8] + ow[8:16] + od[0:8] - code * od[8:16]
         return carry
 
-    acc[...] = jnp.zeros_like(acc)
     lax.fori_loop(0, GROUPS, grad_step, 0)
-    dcs[...] = acc[...].T.reshape(GROUPS, SUB, CODES)
-
-    s_c = block(16)
-    for a, b in FAR_FIRST:
-        other = ((y + a) % 4) * 4 + (z + b) % 4
-        push(dcs.at[other], dcr.at[me], s_c + ((4 - a) % 4) * 4 + (4 - b) % 4, dev_yz(a, b))
+
     dcr[me] = dcs[me]
-    plane_wait(dcr, s_c)
+    for n in range(15):
+        other = (me + 1 + n) % 16
+        arrive(dcr.at[other], s_c + other)
     piece[...] = jnp.sum(dcr[...], axis=0)
 
     s_x = block(4)
@@ -438,6 +486,8 @@
         for h in range(2):
             div_ref[4 * k + 2 * h:4 * k + 2 * h + 2, :] = divb[h, 2 * k:2 * k + 2, :]
 
+    for n in range(15):
+        sends[first_c + n] = (piece_copy(n), None)
     for copy, cond in sends:
         guarded(cond, copy.wait_send)
 
@@ -456,11 +506,12 @@
             pltpu.VMEM((PLANE, QB, D), BF16),
             pltpu.VMEM((2, PB, D), BF16),
             pltpu.VMEM((8, ROWS, TILE), BF16),
-            pltpu.VMEM((CODES, 4 * TILE), BF16),
-            pltpu.VMEM((CODES, 4 * TILE), BF16),
-            pltpu.VMEM((GROUPS, 32, CODES), BF16),
-            pltpu.VMEM((CODES, TILE), F32),
+            pltpu.VMEM((2, PB, TILE), BF16),
+            pltpu.VMEM((4, PB, TILE), BF16),
+            pltpu.VMEM((4, CODES, TILE), BF16),
+            pltpu.VMEM((8, 64, CODES), BF16),
             pltpu.VMEM((GROUPS, SUB, ROWS), F32),
+            pltpu.VMEM((GROUPS, 1, ROWS), F32),
             pltpu.VMEM((GROUPS, CODES, ROWS), BF16),
             pltpu.VMEM((GROUPS, CODES, ROWS), BF16),
             pltpu.VMEM((4, ROWS, 256), F32),
@@ -475,7 +526,10 @@
             pltpu.VMEM((2, 128, TILE), F32),
             pltpu.VMEM((2, ROWS, TILE), F32),
             pltpu.VMEM((2, 128, TILE), F32),
-            pltpu.VMEM((CODES, TILE), F32),
+            pltpu.VMEM((GROUPS, 16, ROWS), BF16),
+            pltpu.VMEM((GROUPS, 1, ROWS), F32),
+            pltpu.VMEM((GROUPS, 16, ROWS), BF16),
+            pltpu.VMEM((4, ROWS, 2 * TILE), BF16),
             pltpu.VMEM((PLANE, SUB, CODES), F32),
             pltpu.VMEM((PLANE, SUB, CODES), F32),
             pltpu.VMEM((SUB, CODES), F32),

time: 78.1 us -> 71.5 us (0.915)
  Pallas kernels: 73.9 us -> 67.3 us
    pallas_call x1, Pallas kernels: 73.9 us -> 67.3 us  [local(): pl.pallas_call(kernel, out_shape=(jax.ShapeDtypeStruct((D, CODES), F32),...]
where the time goes in v3:
time: 71.5 us; the launch traced here: 71.3 us
  Pallas kernels  67.3 us (94%)
  local copies, waits for them, and re-layouts  3.36 us (5%)
    pallas_call x1, Pallas kernels, local(): pl.pallas_call(kernel, out_shape=(jax.ShapeDtypeStruct((D, CODES), F32),...  67.3 us
    unnamed x2, local copies, waits for them, and re-layouts  3.36 us

profile of v3, /device:TPU:1, one launch (start us, length us, event | category | flops | bytes accessed | tf_op | source)
XLA Modules:
  0.0 71.3 jit_solution(5502994251012046845)
XLA Ops:
  0.6 67.3 %shard_map.50 = (f32[768,256]{1,0:T(8,128)}, f32[16,128]{1,0:T(8,128)}) custom-call(bf16[128,768]{1,0:T(8,128)(2,1)} %p_ref.1, bf16[64,768]{1,0:T(8,128)(2,1)} %q_ref.1, f32[768,256]{1,0:T(8,128)} %bitcast.4), custom_call_target="tpu_custom_call" | custom-call | tf_op jit(solution)/shard_map/pallas_call | solution.py:497
  67.9 1.3 %copy.7 = f32[2048]{0:T(1024)} copy(f32[2048]{0:T(1024)} %bitcast.5) | data formatting | bytes 16384
  69.2 2.1 %copy.8 = f32[96,8,256]{2,1,0:T(8,128)} copy(f32[96,8,256]{2,1,0:T(8,128)} %bitcast.3) | data formatting | bytes 1572864

commit v4 on v3

--- a/solution.py
+++ b/solution.py
@@ -23,7 +23,7 @@
 GROUPS = 16
 ROWS = 256
 QN = 1024
-BEFORE = 3
+BEFORE = 4
 N_SEM = 160
 FAR_FIRST = [(2, 2), (2, 1), (2, 3), (1, 2), (3, 2), (1, 1), (1, 3), (3, 1), (3, 3), (2, 0), (0, 2), (1, 0), (3, 0), (0, 1), (0, 3)]
 
@@ -47,8 +47,9 @@
 
 
 def kernel(
-    p_ref, q_ref, cb_ref,
+    p_ref, q_ref, cb_hbm,
     out_ref, div_ref,
+    cb_ref, cb_sem,
     qbuf, pbuf, rbuf,
     xtb, xpack, lhs_f, cp3, rt, inv, a1b, a2b,
     tbuf, ebt, ebs, mloc, stat_t, stat,
@@ -103,9 +104,16 @@
         count[0] += n
         return first
 
+    def tile_col(u_):
+        return pl.multiple_of((3 * core + jnp.minimum(u_, 2)) * TILE, TILE)
+
+    col = tile_col(u)
+    fetch = pltpu.make_async_copy(cb_hbm.at[pl.ds(col, TILE), :], cb_ref, cb_sem)
+    fetch.start()
+
     barrier = pltpu.get_barrier_semaphore()
-    peers = [dev_x(s, c) for s in range(4) for c in (core, 1 - core)][1:]
-    peers += [dev_yz(a, b) for a in range(4) for b in range(4)][1:]
+    peers = [left, right, sibling]
+    peers += [dev_yz(a, b) for a, b in ((0, 1), (0, 3), (0, 2), (1, 0), (3, 0), (2, 0))]
     for peer in peers:
         pl.semaphore_signal(barrier, inc=1, device_id=peer, device_id_type=MESH)
 
@@ -113,11 +121,8 @@
     qbuf[me] = q_ref[...]
     pbuf[xl] = p_ref[...]
 
-    def tile_col(u_):
-        return pl.multiple_of((3 * core + jnp.minimum(u_, 2)) * TILE, TILE)
-
-    col = tile_col(u)
-    cb = cb_ref[pl.ds(col, TILE), :]
+    fetch.wait()
+    cb = cb_ref[...]
     grouped = cb.reshape(GROUPS, SUB, CODES)
     bias = -0.5 * jnp.sum(grouped * grouped, axis=1, keepdims=True)
     b_parts = [jnp.broadcast_to(b.astype(F32), grouped.shape) for b in split3(bias)]
@@ -175,7 +180,7 @@
 
     xtb[xl] = p_ref[:, pl.ds(col, TILE)]
     pack_rows(xl)
-    lax.fori_loop(0, BEFORE, assign_step(xl), 0)
+    lax.fori_loop(0, BEFORE, assign_step(xl), 0, unroll=2)
     pl.semaphore_wait(barrier, len(peers))
 
     def gather_plane(own, piece_of, base):
@@ -223,6 +228,8 @@
                 wait(h, 2, 0, None)
                 for step in (2, 1, 3):
                     send(h, 2, 0, None, False, step)
+
+        def wave2b():
             for h in range(2):
                 for a in (3, 1):
                     for b, part, step in ((3, 0, 1), (1, 1, 3)):
@@ -237,7 +244,7 @@
                 for b in (1, 3, 2):
                     wait(h, 2, b, None)
 
-        return wave0, wave1, wave2, wave3
+        return wave0, wave1, wave2, wave2b, wave3
 
     def q_piece(s, h, part):
         if part is None:
@@ -253,13 +260,13 @@
     qw[0]()
     push(p_ref, pbuf.at[xl], s_p + 1, p_to)
 
-    lax.fori_loop(BEFORE, 8, assign_step(xl), 0)
+    lax.fori_loop(BEFORE, 8, assign_step(xl), 0, unroll=2)
     qw[1]()
     arrive(xtb.at[1 - xl], s_p)
     pack_rows(1 - xl)
-    lax.fori_loop(0, 4, assign_step(1 - xl), 0)
+    lax.fori_loop(0, 4, assign_step(1 - xl), 0, unroll=2)
     qw[2]()
-    lax.fori_loop(4, 8, assign_step(1 - xl), 0)
+    lax.fori_loop(4, 8, assign_step(1 - xl), 0, unroll=2)
 
     mine = core * 4 + u
     rbuf[mine] = rt[...].reshape(TILE, ROWS).T.astype(BF16)
@@ -276,12 +283,13 @@
     for step in (2, 1, 3):
         push(rbuf.at[mine], rbuf.at[mine], s_r + 4 - step, dev_x(step), owner)
     push(rbuf.at[mine], rbuf.at[mine], s_rs, sibling, owner)
+    qw[3]()
     for step in (1, 3, 2):
         s = r_slot(step)
         real = (u + step) % 4 != 3
         arrive(rbuf.at[s], s_r + step, real)
         push(rbuf.at[s], rbuf.at[s], s_rs + step, sibling, real)
-    qw[3]()
+    qw[4]()
     arrive(pbuf.at[1 - xl], s_p + 1)
 
     p_all = pbuf[...].reshape(ROWS, D)
@@ -444,7 +452,7 @@
         d1, d2 = split2((e1.astype(F32) + e2.astype(F32)) * (diff - ts[i]))
         ow = dot(gl[i], e1, NT) + dot(gl[i], e2, NT)
         od = dot(xlt[i], d1, NT) + dot(xlt[i], d2, NT)
-        code = cb_ref[pl.ds(pl.multiple_of(col + SUB * i, SUB), SUB), :]
+        code = cb_ref[pl.ds(pl.multiple_of(SUB * i, SUB), SUB), :]
         dcs[i] = ow[0:8] + ow[8:16] + od[0:8] - code * od[8:16]
         return carry
 
@@ -497,12 +505,14 @@
     grad, divergence = pl.pallas_call(
         kernel,
         out_shape=(
-            jax.ShapeDtypeStruct((D, CODES), F32),
-            jax.ShapeDtypeStruct((16, 128), F32),
+            pltpu.VMEM((D, CODES), F32),
+            pltpu.VMEM((16, 128), F32),
         ),
-        in_specs=[vmem] * 3,
+        in_specs=[vmem, vmem, pl.BlockSpec(memory_space=pl.ANY)],
         out_specs=(vmem, vmem),
         scratch_shapes=[
+            pltpu.VMEM((TILE, CODES), F32),
+            pltpu.SemaphoreType.DMA,
             pltpu.VMEM((PLANE, QB, D), BF16),
             pltpu.VMEM((2, PB, D), BF16),
             pltpu.VMEM((8, ROWS, TILE), BF16),

time: 71.5 us -> 66 us (0.923)
  Pallas kernels: 67.3 us -> 63.8 us
  local copies, waits for them, and re-layouts: 3.36 us -> 1.48 us
    pallas_call x1, Pallas kernels: 67.3 us -> 63.8 us  [local(): pl.pallas_call(kernel, out_shape=(pltpu.VMEM((D, CODES), F32), pltpu.VMEM...]
    unnamed x2, local copies, waits for them, and re-layouts: 3.36 us -> 1.48 us
where the time goes in v4:
time: 66 us; the launch traced here: 65.9 us
  Pallas kernels  63.8 us (97%)
  local copies, waits for them, and re-layouts  1.48 us (2%)
    pallas_call x1, Pallas kernels, local(): pl.pallas_call(kernel, out_shape=(pltpu.VMEM((D, CODES), F32), pltpu.VMEM...  63.8 us
    unnamed x2, local copies, waits for them, and re-layouts  1.48 us

profile of v4, /device:TPU:1, one launch (start us, length us, event | category | flops | bytes accessed | tf_op | source)
XLA Modules:
  0.0 65.9 jit_solution(9878005972668908564)
XLA Ops:
  0.6 63.8 %shard_map.50 = (f32[768,256]{1,0:T(8,128)S(1)}, f32[16,128]{1,0:T(8,128)S(1)}) custom-call(bf16[128,768]{1,0:T(8,128)(2,1)} %p_ref.1, bf16[64,768]{1,0:T(8,128)(2,1)} %q_ref.1, f32[768,256]{1,0:T(8,128)} %bitcast.5), custom_call_target="tpu_custom_call" | custom-call | tf_op jit(solution)/shard_map/pallas_call | solution.py:505
  64.4 0.6 copy.7
  65.0 0.9 %copy.8 = f32[96,8,256]{2,1,0:T(8,128)} copy(f32[96,8,256]{2,1,0:T(8,128)S(1)} %bitcast.3) | data formatting | bytes 1572864

commit v5 on v4

--- a/solution.py
+++ b/solution.py
@@ -24,7 +24,8 @@
 ROWS = 256
 QN = 1024
 BEFORE = 4
-N_SEM = 160
+N_SEM = 224
+LOG2E = 1.4426950408889634
 FAR_FIRST = [(2, 2), (2, 1), (2, 3), (1, 2), (3, 2), (1, 1), (1, 3), (3, 1), (3, 3), (2, 0), (0, 2), (1, 0), (3, 0), (0, 1), (0, 3)]
 
 
@@ -54,7 +55,7 @@
     xtb, xpack, lhs_f, cp3, rt, inv, a1b, a2b,
     tbuf, ebt, ebs, mloc, stat_t, stat,
     gown, gsib, gsrc, rs1, rs2, rs2s,
-    gl, ts, xlt, gpack, dcs, dcr, piece, dbuf, divb,
+    gl, ts, xlt, gpack, dcs, dcr, divb,
     send_sem, recv_sem,
 ):
     qi = lax.axis_index("query")
@@ -294,14 +295,19 @@
 
     p_all = pbuf[...].reshape(ROWS, D)
     scale = float(D) ** (-0.5)
+    scale2 = scale * LOG2E
+    sum_t = []
     for n in range(4):
         qc = qbuf[4 * n:4 * n + 4].reshape(256, D)
-        t = dot(p_all, qc, NT) * scale
+        t = dot(p_all, qc, NT)
         m_t = jnp.max(t, axis=0, keepdims=True)
         tbuf[n] = t
-        e_t = jnp.exp(t - m_t)
+        e_t = jnp.exp2((t - m_t) * scale2)
         ebt[n] = e_t
-        lt = m_t + jnp.log(jnp.sum(e_t, axis=0, keepdims=True))
+        s_t = jnp.sum(e_t, axis=0, keepdims=True)
+        m_t = m_t * scale
+        lt = m_t + jnp.log(s_t)
+        sum_t.append(s_t)
         for k in range(2):
             mloc[2 * n + k:2 * n + k + 1, :] = m_t[:, 128 * k:128 * k + 128]
             stat_t[me, 2 * n + k:2 * n + k + 1, :] = lt[:, 128 * k:128 * k + 128]
@@ -322,14 +328,13 @@
     r_all = jnp.concatenate([rbuf[k] for k in (0, 1, 2, 4, 5, 6)], axis=1)
     for n in range(4):
         qc = qbuf[4 * n:4 * n + 4].reshape(256, D)
-        s = dot(r_all, qc, NT) * scale
+        s = dot(r_all, qc, NT)
         m_s = jnp.max(s, axis=0, keepdims=True)
-        e_s = jnp.exp(s - m_s)
+        e_s = jnp.exp2((s - m_s) * scale2)
         ebs[n] = e_s
+        m_s = m_s * scale
         ls = m_s + jnp.log(jnp.sum(e_s, axis=0, keepdims=True))
-        e_t = ebt[n]
-        cross = jnp.sum(e_t * (tbuf[n] - s), axis=0, keepdims=True)
-        cross = cross / jnp.sum(e_t, axis=0, keepdims=True)
+        cross = jnp.sum(ebt[n] * (tbuf[n] - s), axis=0, keepdims=True) * scale / sum_t[n]
         for k in range(2):
             r = 2 * n + k
             mloc[8 + r:9 + r, :] = m_s[:, 128 * k:128 * k + 128]
@@ -350,9 +355,9 @@
     divb[xl] = cross - big_t + big_s
     s_d = block(1)
     push(divb.at[xl], divb.at[xl], s_d, dev(x + 1 - 2 * xl, y, z, core))
-    f_t = jnp.exp(mloc[0:8, :] - big_t)
-    f_s = jnp.exp(mloc[8:16, :] - big_s)
     weight = (PB * 32 / 64.0) * scale
+    f_t = jnp.exp(mloc[0:8, :] - big_t) * weight
+    f_s = jnp.exp(mloc[8:16, :] - big_s) * weight
 
     grads = []
     for n in range(4):
@@ -360,20 +365,24 @@
             r = 2 * n + k
             cols = slice(128 * k, 128 * k + 128)
             diff = ebs[n, :, cols] * f_s[r:r + 1] - ebt[n, :, cols] * f_t[r:r + 1]
-            grads.append((diff * weight).astype(BF16))
+            grads.append(diff.astype(BF16))
     grad_scores = jnp.concatenate(grads, axis=1)
 
-    def partial(group, d):
-        at = pl.multiple_of(group * 384 + jnp.minimum(d, 2) * TILE, TILE)
-        return dot(grad_scores, qbuf[:, :, pl.ds(at, TILE)].reshape(QN, TILE), NN)
-
-    s_g = block(4)
-    order = (2, 1, 3, 0)
-    for k, step in enumerate(order):
-        gsrc[k] = partial(1 - core, (u + 2 + step) % 4)
-        push(gsrc.at[k], gsib.at[k], s_g + k, sibling)
-    for k, step in enumerate(order):
-        gown[k] = partial(core, (u + step) % 4)
+    def partial(group, first, tiles):
+        at = pl.multiple_of(group * 384 + first * TILE, TILE)
+        return dot(grad_scores, qbuf[:, :, pl.ds(at, TILE * tiles)].reshape(QN, TILE * tiles), NN)
+
+    s_g = block(3)
+    for group, dest in ((1 - core, gsrc), (core, gown)):
+        two = partial(group, 0, 2)
+        dest[0] = two[:, :TILE]
+        dest[1] = two[:, TILE:]
+        if dest is gsrc:
+            push(gsrc.at[0], gsib.at[0], s_g, sibling)
+            push(gsrc.at[1], gsib.at[1], s_g + 1, sibling)
+        dest[2] = partial(group, 2, 1)
+        if dest is gsrc:
+            push(gsrc.at[2], gsib.at[2], s_g + 2, sibling)
 
     s_1 = block(2)
     s_2 = block(4)
@@ -381,31 +390,28 @@
     def half(n):
         return pl.ds(128 * n, 128)
 
-    far_ok = (u + 2) % 4 != 3
-    arrive(gsib.at[0], s_g)
-    gown[0] = gown[0] + gsib[0]
-    for part, to in ((0, right), (1, left)):
-        push(gown.at[0, half(part), :], rs1.at[part], s_1 + part, to, far_ok)
-    for part, to, step in ((0, right, 1), (1, left, 3)):
-        k = 1 + part
+    def near(step):
+        return jnp.minimum((u + step) % 4, 2)
+
+    for k in range(3):
         arrive(gsib.at[k], s_g + k)
         gown[k] = gown[k] + gsib[k]
+    for part, to in ((0, right), (1, left)):
+        push(gown.at[near(2), half(part), :], rs1.at[part], s_1 + part, to, (u + 2) % 4 != 3)
+    for part, to, step in ((0, right, 1), (1, left, 3)):
         push(
-            gown.at[k, half(1 - part), :], rs2.at[part, half(1 - part), :],
+            gown.at[near(step), half(1 - part), :], rs2.at[part, half(1 - part), :],
             s_2 + 2 * part, to, (u + step) % 4 != 3,
         )
-    arrive(gsib.at[3], s_g + 3)
-    gown[3] = gown[3] + gsib[3]
     for part, to, step in ((0, right, 1), (1, left, 3)):
-        k = 1 + part
         ok = (u + step) % 4 != 3
         arrive(rs1.at[part], s_1 + part, ok)
-        rs2s[part] = gown[k, half(part), :] + rs1[part]
+        rs2s[part] = gown[near(step), half(part), :] + rs1[part]
         push(rs2s.at[part], rs2.at[part, half(part), :], s_2 + 2 * part + 1, to, ok)
     for part in range(2):
         arrive(rs2.at[part, half(1 - part), :], s_2 + 2 * part, owner)
         arrive(rs2.at[part, half(part), :], s_2 + 2 * part + 1, owner)
-    g = gown[3] + rs2[0] + rs2[1]
+    g = gown[near(0)] + rs2[0] + rs2[1]
 
     xt = xtb[...].reshape(ROWS, TILE)
     gt = (g.T).reshape(GROUPS, SUB, ROWS) * inv[...]
@@ -421,24 +427,26 @@
         for k in range(4):
             gpack[k, :, TILE * n:TILE * n + TILE] = packs[:, TILE * k:TILE * k + TILE]
 
-    s_c = block(16)
+    s_c = block(64)
     first_c = len(sends)
-    sends.extend([None] * 15)
-
-    def piece_copy(n):
+    sends.extend([None] * 63)
+
+    def piece_copy(n, step):
         other = (me + 1 + n) % 16
         return pltpu.make_async_remote_copy(
-            src_ref=dcs.at[other], dst_ref=dcr.at[me], send_sem=send_sem.at[first_c + n],
-            recv_sem=recv_sem.at[s_c + me], device_id=dev(x, other // 4, other % 4, core),
-            device_id_type=MESH,
+            src_ref=dcs.at[other], dst_ref=dcr.at[u, me],
+            send_sem=send_sem.at[first_c + 4 * n + step - jnp.where(n == 15, 1, 0)],
+            recv_sem=recv_sem.at[s_c + 16 * u + me],
+            device_id=dev((x + step) % 4, other // 4, other % 4, core), device_id_type=MESH,
         )
 
     def grad_step(n, carry):
         i = (me + 1 + n) % 16
 
-        @pl.when(n > 0)
+        @pl.when((n > 0) & owner)
         def _():
-            piece_copy(n - 1).start()
+            for step in range(4):
+                piece_copy(n - 1, step).start()
 
         p, j = i // 4, i % 4
         lp = lhs_f[p]
@@ -458,21 +466,25 @@
 
     lax.fori_loop(0, GROUPS, grad_step, 0)
 
-    dcr[me] = dcs[me]
-    for n in range(15):
-        other = (me + 1 + n) % 16
-        arrive(dcr.at[other], s_c + other)
-    piece[...] = jnp.sum(dcr[...], axis=0)
-
-    s_x = block(4)
-    dbuf[me, mine] = piece[...]
     for step in (2, 1, 3):
-        push(piece, dbuf.at[me, mine], s_x + 4 - step, dev_x(step), owner)
-    for step in (1, 3, 2):
-        arrive(dbuf.at[me, r_slot(step)], s_x + step, (u + step) % 4 != 3)
+        guarded(owner, piece_copy(15, step).start)
+    dcr[u, me] = dcs[me]
+    for k in range(3):
+        arrive(dcr.at[k, me], s_c + 16 * k + me, u != k)
+
+    def piece_wait(n, carry):
+        other = (me + n) % 16
+        for k in range(3):
+            arrive(dcr.at[k, other], s_c + 16 * k + other)
+        return carry
+
+    lax.fori_loop(1, 16, piece_wait, 0)
+
+    for k in range(3):
+        out_ref[3 * core + k, me] = jnp.sum(dcr[k], axis=0)
 
     def trio(s, c):
-        return dbuf.at[s, pl.ds(4 * c, 3), :, :]
+        return out_ref.at[pl.ds(3 * c, 3), s]
 
     s_f = block(16)
     s_fs = block(16)
@@ -485,19 +497,26 @@
         push(trio(s, core), trio(s, core), s_fs + a * 4 + b, sibling)
     for a, b in [(0, 0)] + FAR_FIRST[::-1]:
         arrive(trio(((y + a) % 4) * 4 + (z + b) % 4, 1 - core), s_fs + a * 4 + b)
-    for t in range(6):
-        for p in range(PLANE):
-            out_ref[t * TILE + p * SUB:t * TILE + (p + 1) * SUB, :] = dbuf[p, t + (t // 3)]
 
     arrive(divb.at[1 - xl], s_d)
     for k in range(4):
         for h in range(2):
             div_ref[4 * k + 2 * h:4 * k + 2 * h + 2, :] = divb[h, 2 * k:2 * k + 2, :]
 
-    for n in range(15):
-        sends[first_c + n] = (piece_copy(n), None)
-    for copy, cond in sends:
-        guarded(cond, copy.wait_send)
+    def piece_sent(n, carry):
+        for step in range(4):
+            piece_copy(n, step).wait_send()
+        return carry
+
+    @pl.when(owner)
+    def _():
+        lax.fori_loop(0, 15, piece_sent, 0)
+        for step in (2, 1, 3):
+            piece_copy(15, step).wait_send()
+
+    for entry in sends:
+        if entry is not None:
+            guarded(entry[1], entry[0].wait_send)
 
 
 def local(passages, queries, codebook):
@@ -505,7 +524,7 @@
     grad, divergence = pl.pallas_call(
         kernel,
         out_shape=(
-            pltpu.VMEM((D, CODES), F32),
+            pltpu.VMEM((6, PLANE, SUB, CODES), F32),
             pltpu.VMEM((16, 128), F32),
         ),
         in_specs=[vmem, vmem, pl.BlockSpec(memory_space=pl.ANY)],
@@ -530,9 +549,9 @@
             pltpu.VMEM((16, 128), F32),
             pltpu.VMEM((PLANE, 8, 128), F32),
             pltpu.VMEM((PLANE, 16, 128), F32),
-            pltpu.VMEM((4, ROWS, TILE), F32),
-            pltpu.VMEM((4, ROWS, TILE), F32),
-            pltpu.VMEM((4, ROWS, TILE), F32),
+            pltpu.VMEM((3, ROWS, TILE), F32),
+            pltpu.VMEM((3, ROWS, TILE), F32),
+            pltpu.VMEM((3, ROWS, TILE), F32),
             pltpu.VMEM((2, 128, TILE), F32),
             pltpu.VMEM((2, ROWS, TILE), F32),
             pltpu.VMEM((2, 128, TILE), F32),
@@ -541,12 +560,10 @@
             pltpu.VMEM((GROUPS, 16, ROWS), BF16),
             pltpu.VMEM((4, ROWS, 2 * TILE), BF16),
             pltpu.VMEM((PLANE, SUB, CODES), F32),
-            pltpu.VMEM((PLANE, SUB, CODES), F32),
-            pltpu.VMEM((SUB, CODES), F32),
-            pltpu.VMEM((PLANE, 8, SUB, CODES), F32),
+            pltpu.VMEM((4, PLANE, SUB, CODES), F32),
             pltpu.VMEM((2, 8, 128), F32),
             pltpu.SemaphoreType.DMA((N_SEM,)),
-            pltpu.SemaphoreType.DMA((200,)),
+            pltpu.SemaphoreType.DMA((240,)),
         ],
         compiler_params=pltpu.CompilerParams(
             collective_id=0, has_side_effects=True, vmem_limit_bytes=60 * 1024 * 1024

time: 66 us -> 65.6 us (level)
  no operation moved by 1% of the time
where the time goes in v5:
time: 65.6 us; the launch traced here: 65.5 us
  Pallas kernels  63.4 us (97%)
  local copies, waits for them, and re-layouts  1.48 us (2%)
    pallas_call x1, Pallas kernels, local(): pl.pallas_call(kernel, out_shape=(pltpu.VMEM((6, PLANE, SUB, CODES), F32)...  63.4 us
    unnamed x2, local copies, waits for them, and re-layouts  1.48 us

profile of v5, /device:TPU:1, one launch (start us, length us, event | category | flops | bytes accessed | tf_op | source)
XLA Modules:
  0.0 65.5 jit_solution(9121418557786072286)
XLA Ops:
  0.6 63.4 %shard_map.50 = (f32[6,16,8,256]{3,2,1,0:T(8,128)S(1)}, f32[16,128]{1,0:T(8,128)S(1)}) custom-call(bf16[128,768]{1,0:T(8,128)(2,1)} %p_ref.1, bf16[64,768]{1,0:T(8,128)(2,1)} %q_ref.1, f32[768,256]{1,0:T(8,128)} %bitcast.5), custom_call_target="tpu_custom_call" | custom-call | tf_op jit(solution)/shard_map/pallas_call | solution.py:524
  64.0 0.6 copy.7
  64.6 0.9 %copy.8 = f32[96,8,256]{2,1,0:T(8,128)} copy(f32[96,8,256]{2,1,0:T(8,128)S(1)} %bitcast.3) | data formatting | bytes 1572864
